TPU v7x, 256 devices: a whole 4x4x8 slice. The times are simulated.
256 devices in a mesh: cable: 4 (over y), fx: 32 (over z, x), fz: 2 (over core).
Axes of the slice: x: 4, y: 4, z: 8, core: 2. Of those that a mesh axis runs over, the one named last changes fastest.
Arguments:
- velocity: float32 [3, 256, 64, 256], P(None, 'fx', 'cable', 'fz'), may hold values from -6 to 6
- viscosity: float32 [256, 64, 256], P('fx', 'cable', 'fz'), may hold values from 0.02 to 0.15
- disp_init: float32 [3, 16384], P(None, ('cable', 'fx', 'fz')), may hold values from -3 to 3
- rest_shape: float32 [3, 16384], P(None, ('cable', 'fx', 'fz')), may hold values from -6 to 6
- compliance: float32 [16384], P(('cable', 'fx', 'fz')), may hold values from 0.5 to 2
- stencil_weights: float32 [3, 12, 16384], P(None, None, ('cable', 'fx', 'fz')), may hold values from 0.05 to 0.45
- anchor: int32 [3, 16384], P(None, ('cable', 'fx', 'fz')), may hold values from 0 to 9852, as said below
- owners: int32 [3, 16384], P(None, ('cable', 'fx', 'fz')), may hold values from 0 to 63, as said below
Outputs:
- disp_next: float32 [3, 16384], P(None, ('cable', 'fx', 'fz'))
- velocity_out: float32 [3, 256, 64, 256], P(None, 'fx', 'cable', 'fz')
Inputs may be any that keep to these rules, and one draw needn't show every extreme that they name: `owners`: the owner's number is fx * 2 + fz of a fluid block in the segment's own cable group. Among the 64 segments of one device (aligned blocks of 64 segments), at most 4 name the same owner in one iteration; in every iteration one owner is named by exactly 4 segments of every device of each group. `anchor`: the cell is numbered (x * 16 + y) * 128 + z in the owner's block, with x <= 4, y <= 12 and z <= 124, so the 4 x 4 x 4 stencil lies inside that block.
All inputs are finite; a program needn't handle non-finite values.
Results may differ from a plain program's by a relative error of at most 0.0003.
Values sent between devices are 32-bit elements; how exact they have to be, the bound alone decides.
No kernel may reach another device: no remote copies, remote signals or barrier semaphores. Data moves between devices by JAX's collectives and lax.ppermute only.
A program may use at most 64 MiB of HBM per device.

v0:
```python
import functools

import jax
import jax.numpy as jnp
from jax import lax
from jax.experimental import pallas as pl
from jax.experimental.pallas import tpu as pltpu
from jax.sharding import PartitionSpec as P


F32 = jnp.float32
BF16 = jnp.bfloat16
NT = (((1,), (1,)), ((), ()))
NN = (((1,), (0,)), ((), ()))

spread_gain = 16.0
drag_coeff = 0.05
relaxation = 0.5
ridge_share = 0.01

SEG_DEV = 64
GROUP = 64
CAP = 4
HALF = GROUP // 2
SLOTS = GROUP * CAP
SX, SY, SZ = 8, 16, 128
XY = SX * SY

R_W, R_CELL, R_D0, R_REST, R_CR, R_CODE = 0, 12, 13, 16, 19, 20
HEIGHT = (16, 24, 24)
SETS = 3
BASE = (0, 0, 288)
EARLY, LATE = 256, 640


def split(x):
    hi = x.astype(BF16)
    return hi, (x - hi.astype(F32)).astype(BF16)


def dot(a, b, dims):
    return lax.dot_general(a, b, dims, preferred_element_type=F32)


def iota(shape, dim):
    return lax.broadcasted_iota(jnp.int32, shape, dim)


def split3(x):
    hi, low = split(x)
    return hi, low, (x - hi.astype(F32) - low.astype(F32)).astype(BF16)


def rank_of(own):
    hot = (iota((GROUP, SEG_DEV), 0) == own).astype(F32)
    earlier = (iota((SEG_DEV, SEG_DEV), 0) < iota((SEG_DEV, SEG_DEV), 1)).astype(F32)
    return jnp.sum(hot * dot(hot, earlier, NN), axis=0, keepdims=True)


def put_slots(fields, rank, rows, turn, base):
    height = fields.shape[0]
    parts = split3(jnp.concatenate([jnp.where(rank == k, fields, 0.0) for k in range(CAP)], axis=0))
    dest = iota((GROUP, SEG_DEV), 0)
    hots = jnp.concatenate([(dest == row).astype(F32).astype(BF16) for row in rows], axis=0)
    got = dot(parts[0], hots, NT) + (dot(parts[1], hots, NT) + dot(parts[2], hots, NT))
    for j in range(SETS):
        start = base + CAP * height * j
        turn[start : start + CAP * height, 0:GROUP] = got[:, GROUP * j : GROUP * (j + 1)]


def pack_kernel(*refs):
    far, (msg, later, firsts, xlo, xhi), near, (turn, sems) = refs[0:7], refs[7:12], refs[12:18], refs[18:20]
    copies = [pltpu.make_async_copy(far[n], near[n], sems.at[n]) for n in (5, 4, 3, 0, 1, 2)]
    copies.append(pltpu.make_async_copy(far[6].at[:, 0:SY, :], xlo, sems.at[6]))
    copies.append(pltpu.make_async_copy(far[6].at[:, XY - SY : XY, :], xhi, sems.at[7]))
    for copy in copies:
        copy.start()
    disp, rest, comp, weights, anchor, owner = near
    fz_n, fx_n, cable_n = lax.axis_size("fz"), lax.axis_size("fx"), lax.axis_size("cable")
    device = (lax.axis_index("cable") * fx_n + lax.axis_index("fx")) * fz_n + lax.axis_index("fz")
    position = (device * SEG_DEV + iota((1, SEG_DEV), 1)).astype(F32)
    ramp = 1.0 + 2.0 * position / (SEG_DEV * fz_n * fx_n * cable_n)
    later[...] = jnp.zeros_like(later)
    firsts[...] = jnp.zeros_like(firsts)
    turn[...] = jnp.zeros_like(turn)
    for copy in copies:
        copy.wait()
    own = owner[0:1, :]
    rank = rank_of(own)
    firsts[0:12, :] = weights[0]
    firsts[R_CELL : R_CELL + 1, :] = anchor[0:1, :].astype(F32)
    firsts[R_D0 : R_D0 + 3, :] = disp[...]
    put_slots(firsts[0 : HEIGHT[0], :], rank, (own, own + fz_n, own - fz_n), turn, BASE[0])
    for n in range(EARLY // 128):
        msg[:, 128 * n : 128 * n + 128] = jnp.transpose(turn[128 * n : 128 * n + 128, :])[0:GROUP]
    for t in (1, 2):
        at = 24 * (t - 1)
        later[at : at + 12, :] = weights[t]
        later[at + R_CELL : at + R_CELL + 1, :] = anchor[t : t + 1, :].astype(F32)
        later[at + R_D0 : at + R_D0 + 3, :] = disp[...]
        later[at + R_REST : at + R_REST + 3, :] = rest[...]
        later[at + R_CR : at + R_CR + 1, :] = comp[...] * ramp
    later[48:51, :] = owner[...].astype(F32)
    later[51:52, :] = rank


def pack_later_kernel(later, keep, give, place, turn):
    mine = lax.axis_index("fz")
    turn[...] = jnp.zeros_like(turn)
    owners = [later[48 + t : 49 + t, :].astype(jnp.int32) for t in range(3)]
    ranks = [later[51:52, :], rank_of(owners[1]), rank_of(owners[2])]
    codes = [owners[t].astype(F32) * CAP + ranks[t] for t in range(2)]
    code = codes[0] + SLOTS * codes[1]
    for t in (1, 2):
        side, fx = (owners[t] & 1) ^ mine, owners[t] >> 1
        at = side * HALF + fx
        rows = (at, jnp.where(fx < HALF - 1, at + 1, -1), jnp.where(fx > 0, at - 1, -1))
        fields = later[24 * (t - 1) : 24 * t, :]
        fields = jnp.where(iota((24, SEG_DEV), 0) == R_CODE, code, fields)
        put_slots(fields, ranks[t], rows, turn, BASE[t])
    for n in range(LATE // 128):
        lanes = slice(128 * n, 128 * n + 128)
        block = jnp.transpose(turn[lanes, :])
        keep[:, lanes] = block[0:HALF]
        give[:, lanes] = block[HALF:GROUP]
    place[...] = jnp.zeros_like(place)
    place[0:1, :] = later[50:51, :]
    place[1:2, :] = ranks[2]


def turn_static(static, turned, t):
    first = BASE[t] // 128
    last = (BASE[t] + SETS * CAP * HEIGHT[t] + 127) // 128
    low = lax.axis_index("fz") == 0
    for n in range(first, last):
        if t == 0:
            spare = LATE - GROUP
            turned[spare:LATE, :] = static[:, 128 * n : 128 * n + 128]
            homes = [turned[pl.ds(spare + f, HALF, stride=2), :] for f in range(2)]
        else:
            at = 3 * SLOTS + 128 * n
            same, other = static[:, at : at + 128], static[:, at + LATE : at + LATE + 128]
            homes = [jnp.where(low, same, other), jnp.where(low, other, same)]
        wide = jnp.concatenate([*homes, jnp.zeros((128 - GROUP, 128), F32)], axis=0)
        turned[128 * n : 128 * n + 128, :] = jnp.transpose(wide)


def slot_rows(turned, t, j):
    height = HEIGHT[t]
    start = BASE[t] + CAP * height * j
    part = [turned[start + height * k : start + height * (k + 1), :] for k in range(CAP)]
    halves = [part[2 * n] + pltpu.roll(part[2 * n + 1], 64, 1) for n in range(2)]
    return jnp.concatenate(halves, axis=1)


def along(rows, first, at):
    total = jnp.zeros(at.shape, F32)
    for i in range(4):
        total = jnp.where(at == i, rows[first + i : first + i + 1], total)
    return total


def tables(rows, plane=None):
    cell = rows[R_CELL : R_CELL + 1].astype(jnp.int32)
    wy = along(rows, R_W + 4, iota((SY, SLOTS), 0) - ((cell >> 7) & (SY - 1)))
    wz = along(rows, R_W + 8, iota((SZ, SLOTS), 0) - (cell & (SZ - 1)))
    if plane is not None:
        return along(rows, R_W, plane - (cell >> 11)) * wy, wz
    wx = along(rows, R_W, iota((SX, SLOTS), 0) - (cell >> 11))
    return jnp.concatenate([wx[x : x + 1] * wy for x in range(SX)], axis=0), wz


def spread(wxy, wz2, base):
    hi, low = split(jnp.concatenate([wxy * (spread_gain * base[c]) for c in range(3)], axis=0))
    both = dot(hi, wz2, NT)
    return both[:, :SZ] + (both[:, SZ:] + dot(low, wz2[0:SZ], NT))


def look_up(halves, code):
    low_half = iota((1, 128), 1) < 64
    mine = lax.axis_index("fz")
    height = HALF
    label = (iota((height, SLOTS), 0) * 2 + mine) * CAP + iota((height, SLOTS), 1) // 64
    labels = (label, label + CAP * (1 - 2 * mine))
    found = [[None] * 2 for _ in range(3)]
    for part in range(2):
        piece = code[:, 128 * part : 128 * part + 128]
        turned = pltpu.roll(piece, 64, 1)
        pair = []
        for odd in range(2):
            both = jnp.where(low_half, turned, piece) if odd else jnp.where(low_half, piece, turned)
            wanted = jnp.concatenate([both, both], axis=1)
            per = []
            for comp in range(3):
                lanes = slice(comp * SLOTS, (comp + 1) * SLOTS)
                hit = jnp.where(labels[0] == wanted, halves[0][:, lanes], 0.0)
                hit = hit + jnp.where(labels[1] == wanted, halves[1][:, lanes], 0.0)
                hit = jnp.sum(hit, axis=0, keepdims=True)
                hit = hit[:, :128] + hit[:, 128:]
                per.append(hit + pltpu.roll(hit, 64, 1))
            pair.append(per)
        for comp in range(3):
            found[comp][part] = jnp.where(low_half, pair[0][comp], pair[1][comp])
    return [jnp.concatenate(found[comp], axis=1) for comp in range(3)]


def responses(rows, sampled):
    cr = rows[R_CR : R_CR + 1]
    return [rows[R_REST + c : R_REST + c + 1] + cr * sampled[c] for c in range(3)]


def prepare_kernel(t, *refs):
    static, sent, (wxy_out, wz_out, plane_out, slots, turned) = refs[0], refs[1:-5], refs[-5:]
    turn_static(static, turned, t)
    for j in range(SETS):
        rows = slot_rows(turned, t, j)
        wxy, wz = tables(rows, (None, SX - 1, 0)[j])
        hi, low = split(wz)
        wz_out[j, 0:SZ, :] = hi
        wz_out[j, SZ:, :] = low
        if j == 0:
            wxy_out[...] = wxy
        else:
            plane_out[j - 1] = wxy
        slots[32 * j : 32 * j + HEIGHT[t], :] = rows
        if t == 2:
            code = rows[R_CODE : R_CODE + 1].astype(jnp.int32)
            before = responses(rows, look_up(sent, code & (SLOTS - 1)))
            for c in range(3):
                slots[32 * j + 24 + c : 32 * j + 25 + c, :] = before[c]


def displacements(t, rows, sent):
    first = [rows[R_D0 + c : R_D0 + c + 1] for c in range(3)]
    if t == 0:
        return [first], []
    code = rows[R_CODE : R_CODE + 1].astype(jnp.int32)
    if t == 1:
        before = responses(rows, look_up(sent, code & (SLOTS - 1)))
    else:
        before = [rows[24 + c : 25 + c] for c in range(3)]
    gap = [before[c] - first[c] for c in range(3)]
    second = [first[c] + relaxation * gap[c] for c in range(3)]
    if t == 1:
        return [second], [second, gap]
    latest = responses(rows, look_up(sent, code >> 8))
    change = [latest[c] - before[c] for c in range(3)]
    return [latest, change], [latest, change, gap, [latest[c] - second[c] for c in range(3)], before]


def spread_kernel(t, *refs):
    if t == 0:
        static, velocity = refs[0:2]
        sent = ()
        field, xl, xu, ylo, yhi, *tabled, turned = refs[2:]
        prepare_kernel(0, static, *tabled, turned)
    else:
        velocity, sent, tabled = refs[0], refs[1:3], refs[3:7]
        field, xl, xu, ylo, yhi, aux = refs[7:13]
        aux[...] = jnp.zeros_like(aux)
    wxy, wz, plane, slots = tabled
    for j, out in enumerate((field, xl, xu)):
        rows = slots[32 * j : 32 * j + 32, :]
        bases, kept = displacements(t, rows, sent)
        height = SY if j else XY
        for n, base in enumerate(bases):
            forced = spread(plane[j - 1] if j else wxy[...], wz[j], base)
            for c in range(3):
                part = forced[height * c : height * (c + 1)]
                out[3 * n + c] = part + velocity[c] if n == 0 and j == 0 else part
        if j == 0 and t > 0:
            for n, group in enumerate(kept):
                for c in range(3):
                    aux[3 * n + c : 3 * n + c + 1, :] = group[c]
            aux[16:20, :] = rows[R_REST : R_REST + 4]
    for n in range(3 * len(bases)):
        ylo[n] = field[n, pl.ds(0, SX, stride=SY), :]
        yhi[n] = field[n, pl.ds(SY - 1, SX, stride=SY), :]
    if t == 2:
        lanes = slice(3 * SLOTS, 3 * SLOTS + 128)
        total = jnp.sum(sent[0][:, lanes] + sent[1][:, lanes], axis=0, keepdims=True)
        total = jnp.broadcast_to(total, (8, 128))
        ylo[6] = total
        yhi[6] = total
        refs[13][...] = total


def wake(u, beside_z, xl, xu, yl, yu, viscosity):
    lane = iota((XY, SZ), 1)
    y = iota((XY, SZ), 0) % SY
    upper_core = lax.axis_index("fz") > 0
    speed = jnp.sqrt(1.0 + (u[0] * u[0] + u[1] * u[1] + u[2] * u[2]))
    new = []
    for c in range(3):
        here = u[c]
        near = jnp.concatenate([xl[c], here[: XY - SY]], axis=0)
        near = near + jnp.concatenate([here[SY:], xu[c]], axis=0)
        wide_l = jnp.concatenate([jnp.broadcast_to(yl[c][x : x + 1], (SY, SZ)) for x in range(SX)], axis=0)
        wide_u = jnp.concatenate([jnp.broadcast_to(yu[c][x : x + 1], (SY, SZ)) for x in range(SX)], axis=0)
        near = near + jnp.where(y == 0, wide_l, pltpu.roll(here, 1, 0))
        near = near + jnp.where(y == SY - 1, wide_u, pltpu.roll(here, XY - 1, 0))
        left = jnp.where(upper_core, beside_z[c], 0.0)
        right = jnp.where(upper_core, 0.0, beside_z[c])
        near = near + pltpu.roll(jnp.where(lane == SZ - 1, left, here), 1, 1)
        near = near + pltpu.roll(jnp.where(lane == 0, right, here), SZ - 1, 1)
        new.append(here + viscosity * (near - 6.0 * here) - drag_coeff * here * speed)
    return new


def sample(new, wxy, wz2):
    wz_hi, wz_low = wz2[0:SZ], wz2[SZ:]
    both = jnp.concatenate([wz_hi, wz_hi], axis=0)
    sampled = []
    for c in range(3):
        hi, low = split(new[c])
        along_z = dot(jnp.concatenate([hi, low], axis=1), both, NN) + dot(hi, wz_low, NN)
        sampled.append(jnp.sum(wxy * along_z, axis=0, keepdims=True))
    return sampled


def product(a, b):
    rows = a[0] * b[0] + a[1] * b[1] + a[2] * b[2]
    return rows[:, :128] + rows[:, 128:]


def lane_of(row, n):
    return jnp.sum(jnp.where(iota(row.shape, 1) == n, row, 0.0), axis=1, keepdims=True)


def sample_kernel(t, *refs):
    viscosity, far_l, far_u = refs[0:3]
    refs = refs[2:]
    field, beside_z, xl, xu, yl, yu, wxy, wz = refs[1:9]
    fx = lax.axis_index("fx")
    me = lax.axis_index("cable")
    last = lax.axis_size("cable") - 1

    def whole(ref):
        if t < 2:
            return [ref[c] for c in range(3)]
        return [ref[c] + coef * ref[3 + c] for c in range(3)]

    if t == 2:
        gram = yl[6] + yu[6] + (refs[10][...] + refs[11][...])
        first = iota((1, 128), 1) < 64
        square = jnp.sum(jnp.where(first, gram[0:1], 0.0), axis=1, keepdims=True)
        target = jnp.sum(jnp.where(first, 0.0, gram[0:1]), axis=1, keepdims=True)
        coef = -target / (square + (ridge_share * square + 1e-06))
    u = whole(field)
    below = [jnp.where(me > 0, face, 0.0) for face in whole(yl)]
    above = [jnp.where(me < last, face, 0.0) for face in whole(yu)]
    before = [jnp.where(fx > 0, far_l[c], 0.0) + part for c, part in enumerate(whole(xl))]
    after = [jnp.where(fx < lax.axis_size("fx") - 1, far_u[c], 0.0) + part for c, part in enumerate(whole(xu))]
    faces = [before, after, below, above]
    new = wake(u, whole(beside_z), *faces, viscosity[...])
    sampled = sample(new, wxy[...], wz[0])
    if t == 0:
        keep, got, msg = refs[9:12]
        for c in range(3):
            msg[:, SLOTS * c : SLOTS * (c + 1)] = jnp.broadcast_to(sampled[c], (HALF, SLOTS))
        msg[:, 3 * SLOTS : 3 * SLOTS + LATE] = keep[...]
        msg[:, 3 * SLOTS + LATE :] = got[...]
        return
    aux = refs[9]

    def kept(n):
        return [aux[3 * n + c : 3 * n + c + 1, :] for c in range(3)]

    cr = aux[19:20, :]
    response = [aux[16 + c : 17 + c, :] + cr * sampled[c] for c in range(3)]
    if t == 1:
        msg = refs[10]
        disp, gap0 = kept(0), kept(1)
        gap = [response[c] - disp[c] for c in range(3)]
        v0 = [gap[c] - gap0[c] for c in range(3)]
        for c in range(3):
            msg[:, SLOTS * c : SLOTS * (c + 1)] = jnp.broadcast_to(sampled[c], (HALF, SLOTS))
        square, target = product(v0, v0), product(v0, gap)
        square, target = (part + pltpu.roll(part, 64, 1) for part in (square, target))
        row = jnp.where(iota((1, 128), 1) < 64, square, target)
        msg[:, 3 * SLOTS : 3 * SLOTS + 128] = jnp.broadcast_to(row, (HALF, 128))
        return
    out, msg, turn = refs[12:15]
    for c in range(3):
        out[c] = new[c]
    latest, change, gap0, gap1, before = (kept(n) for n in range(5))
    disp = [latest[c] + coef * change[c] for c in range(3)]
    gap = [response[c] - disp[c] for c in range(3)]
    v0 = [gap[c] - gap0[c] for c in range(3)]
    v1 = [gap[c] - gap1[c] for c in range(3)]
    turn[...] = jnp.zeros_like(turn)
    for n, group in enumerate((response, before, latest)):
        for c in range(3):
            turn[3 * n + c : 3 * n + c + 1, :] = group[c][:, :128]
            turn[32 + 3 * n + c : 33 + 3 * n + c, :] = group[c][:, 128:]
    for n, (a, b) in enumerate(((v0, v0), (v0, v1), (v1, v1), (v0, gap), (v1, gap))):
        turn[64 + n : 65 + n, :] = product(a, b)
    turned = jnp.transpose(turn[...])
    row = jnp.sum(turned, axis=0, keepdims=True)
    block = turned[0:64] + pltpu.roll(turned[64:128], 16, 1)
    block = jnp.where(iota((1, 128), 1) < 64, block, row)
    for c in range(4):
        for f in range(2):
            msg[pl.ds(GROUP * c + f, HALF, stride=2), :] = block[HALF * f : HALF * (f + 1)]


def finish_kernel(sent, place, out):
    row = jnp.sum(sent[...], axis=0, keepdims=True)
    g00, g01, g11, b0, b1 = (lane_of(row, 64 + n) for n in range(5))
    shift = ridge_share * (g00 + g11) / 2 + 1e-06
    first, second = g00 + shift, g11 + shift
    determinant = first * second - g01 * g01
    c0 = -(second * b0 - g01 * b1) / determinant
    c1 = -(first * b1 - g01 * b0) / determinant
    start = pl.multiple_of(lax.axis_index("cable") * GROUP, GROUP)
    mine = sent[pl.ds(start, GROUP), :]
    turned = jnp.transpose(jnp.concatenate([mine, jnp.zeros((128 - GROUP, 128), F32)], axis=0))
    hot = (iota((128, SEG_DEV), 0).astype(F32) == place[0:1, :]).astype(F32).astype(BF16)
    parts = split3(turned[0:64])
    got = dot(parts[0], hot, NN) + (dot(parts[1], hot, NN) + dot(parts[2], hot, NN))
    rank = place[1:2, :]
    rows = jnp.zeros((16, SEG_DEV), F32)
    for k in range(CAP):
        rows = jnp.where(rank == k, got[16 * k : 16 * k + 16], rows)
    response, before, latest = rows[0:3], rows[3:6], rows[6:9]
    out[...] = response + c0 * (response - before) + c1 * (response - latest)


def shape(*dims, kind=F32):
    return jax.ShapeDtypeStruct(dims, kind)


def call(kernel, ins, outs, scratch=(), space=pltpu.VMEM):
    size = sum(a.size * a.dtype.itemsize for a in (*ins, *outs))
    return pl.pallas_call(
        kernel,
        out_shape=outs,
        in_specs=[pl.BlockSpec(memory_space=space)] * len(ins),
        out_specs=[pl.BlockSpec(memory_space=pltpu.VMEM)] * len(outs),
        scratch_shapes=list(scratch),
        compiler_params=pltpu.CompilerParams(vmem_limit_bytes=16 * 1024 * 1024),
        cost_estimate=pl.CostEstimate(flops=0, bytes_accessed=size, transcendentals=0),
    )(*ins)


def shifted(array, axis, by):
    count = lax.axis_size(axis)
    return lax.ppermute(array, axis, [(i, (i + by) % count) for i in range(count)])


def exchange(array, axes):
    return lax.all_to_all(array, axes, 0, 0, tiled=True)


def body(velocity, viscosity, disp_init, rest_shape, compliance, stencil_weights, anchor, owners):
    flow = velocity.reshape(3, XY, SZ)
    thick = viscosity.reshape(XY, SZ)
    ins = (disp_init, rest_shape, compliance.reshape(1, SEG_DEV), stencil_weights, anchor, owners)
    msg, later, _, xlo, xhi = call(
        pack_kernel,
        tuple(pltpu.with_memory_space_constraint(a, pltpu.HBM) for a in (*ins, flow)),
        [shape(GROUP, EARLY), shape(56, SEG_DEV), shape(24, SEG_DEV), shape(3, SY, SZ), shape(3, SY, SZ)],
        [pltpu.VMEM(a.shape, a.dtype) for a in ins]
        + [pltpu.VMEM((EARLY, 128), F32), pltpu.SemaphoreType.DMA((8,))],
        pltpu.HBM,
    )
    static = exchange(msg, ("fx", "fz"))
    far_l = shifted(xhi, "fx", 1)
    far_u = shifted(xlo, "fx", -1)
    keep, give, place = call(
        pack_later_kernel,
        (later,),
        [shape(HALF, LATE), shape(HALF, LATE), shape(8, SEG_DEV)],
        [pltpu.VMEM((LATE, 128), F32)],
    )
    static, *carried = lax.optimization_barrier((static, keep, shifted(give, "fz", 1)))
    table_outs = [
        shape(XY, SLOTS),
        shape(SETS, 2 * SZ, SLOTS, kind=BF16),
        shape(2, SY, SLOTS),
        shape(32 * SETS, SLOTS),
    ]
    turned = [pltpu.VMEM((LATE, 128), F32)]
    sent, tabled = (), ()
    for t in range(3):
        n = 6 if t == 2 else 3
        faced = 7 if t == 2 else 3
        outs = [shape(n, XY, SZ), shape(n, SY, SZ), shape(n, SY, SZ)] + [shape(faced, SX, SZ)] * 2
        kernel = functools.partial(spread_kernel, t)
        if t == 0:
            field, xl, xu, ylo, yhi, *tabled = call(kernel, (static, flow), outs + table_outs, turned)
            extra = []
        else:
            outs.append(shape(24, SLOTS))
            if t == 2:
                outs.append(shape(8, 128))
            field, xl, xu, ylo, yhi, *extra = call(kernel, (flow, *sent, *tabled), outs)
        yl = shifted(yhi, "cable", 1)
        yu = shifted(ylo, "cable", -1)
        beside_z = shifted(field, "fz", 1)
        if t == 2:
            across = shifted(extra[1], "cable", 2)
        ins = [thick, far_l, far_u, field, beside_z, xl, xu, yl, yu, *tabled[0:2], *extra]
        kernel = functools.partial(sample_kernel, t)
        if t < 2:
            if t == 0:
                ins += carried
            (msg,) = call(kernel, ins, [shape(HALF, 3 * SLOTS + (128 if t else 2 * LATE))])
            half = exchange(msg, "fx")
            if t == 0:
                static, before = half, ()
            sent = (half, shifted(half if t else half[:, : 3 * SLOTS], "fz", 1))
            tabled = call(functools.partial(prepare_kernel, t + 1), (static, *before), table_outs, turned)
            before = sent
        else:
            ins.append(across)
            out, msg = call(kernel, ins, [shape(3, XY, SZ), shape(4 * GROUP, 128)], [pltpu.VMEM((128, 128), F32)])
    last = exchange(msg, ("cable", "fx", "fz"))
    (disp_next,) = call(finish_kernel, (last, place), [shape(3, SEG_DEV)])
    return disp_next, out.reshape(velocity.shape)


def solution(mesh):
    segments = ("cable", "fx", "fz")
    placed = (
        P(None, "fx", "cable", "fz"),
        P("fx", "cable", "fz"),
        P(None, segments),
        P(None, segments),
        P(segments),
        P(None, None, segments),
        P(None, segments),
        P(None, segments),
    )
    return jax.shard_map(
        body,
        mesh=mesh,
        in_specs=placed,
        out_specs=(P(None, segments), P(None, "fx", "cable", "fz")),
        check_vma=False,
    )
```

profile of v0, /device:TPU:1, one launch (start us, length us, event | category | flops | bytes accessed | tf_op | source)
XLA Modules:
  0.0 107.2 jit_solution(4529592089318107090)
XLA Ops:
  0.6 1.5 %shard_map.95 = (f32[64,256]{1,0:T(8,128)S(1)}, f32[56,64]{1,0:T(8,128)S(1)}, f32[24,64]{1,0:T(8,128)}, f32[3,16,128]{2,1,0:T(8,128)S(1)}, f32[3,16,128]{2,1,0:T(8,128)S(1)}) custom-call(f32[3,64]{1,0:T(4,128)} %refs_0_.1, f32[3,64]{1,0:T(4,128)} %refs_1_.1, f32[1,64]{1,0:T(1,128)} %bitcast.40, f32[3,12,64]{2,1,0:T(8,128)} %refs_3_.1, s32[3,64]{1,0:T(4,128)} %refs_4_.1, ...), custom_call_target="tpu_custom_call" | custom-call | bytes 344320 | tf_op jit(solution)/shard_map/pallas_call | solution.py:435
  2.2 0.0 copy-start
  2.2 0.7 copy.10
  2.9 13.0 %all-to-all-start = ((f32[64,1,256]{2,1,0:T(1,128)}), f32[64,1,256]{2,1,0:T(1,128)S(1)}, u32[]{:S(2)}, u32[]{:S(2)}) async-start(f32[64,1,256]{2,1,0:T(1,128)} %copy.10), calls=%async_computation | async-start | bytes 131072 | tf_op jit(solution)/shard_map/all_to_all | solution.py:452
  15.9 0.6 shard_map.96
  16.5 0.5 collective-permute-start.2
  17.0 8.9 %all-to-all-done = f32[64,1,256]{2,1,0:T(1,128)S(1)} async-done(((f32[64,1,256]{2,1,0:T(1,128)}), f32[64,1,256]{2,1,0:T(1,128)S(1)}, u32[]{:S(2)}, u32[]{:S(2)}) %all-to-all-start) | async-done | bytes 65568 | tf_op jit(solution)/shard_map/all_to_all | solution.py:452
  26.0 0.0 copy-start.1
  26.0 1.0 shard_map.97
  27.0 0.4 collective-permute-start.3
  27.4 0.2 collective-permute-start
  27.6 4.6 %collective-permute-start.1 = (f32[3,16,128]{2,1,0:T(8,128)S(1)}, f32[3,16,128]{2,1,0:T(8,128)S(1)}, u32[]{:S(2)}, u32[]{:S(2)}) collective-permute-start(f32[3,16,128]{2,1,0:T(8,128)S(1)} %get-tuple-element.43), channel_id=1, source_target_pairs={{0,62},{2,0},{4,2},{6,4},{8,6},{10,8},{12,10},{14,12},{16,14},{18,... | collective-permute-start | bytes 73736 | tf_op jit(solution)/shard_map/ppermute | solution.py:448
  32.2 1.3 %collective-permute-start.4 = (f32[3,8,128]{2,1,0:T(8,128)S(1)}, f32[3,8,128]{2,1,0:T(8,128)S(1)}, u32[]{:S(2)}, u32[]{:S(2)}) collective-permute-start(f32[3,8,128]{2,1,0:T(8,128)S(1)} %get-tuple-element.52), channel_id=1, source_target_pairs={{0,64},{64,128},{128,192},{192,0},{1,65},{65,129},{129,193},{193,1... | collective-permute-start | bytes 36872 | tf_op jit(solution)/shard_map/ppermute | solution.py:448
  33.5 1.4 %collective-permute-start.5 = (f32[3,8,128]{2,1,0:T(8,128)S(1)}, f32[3,8,128]{2,1,0:T(8,128)S(1)}, u32[]{:S(2)}, u32[]{:S(2)}) collective-permute-start(f32[3,8,128]{2,1,0:T(8,128)S(1)} %get-tuple-element.53), channel_id=1, source_target_pairs={{0,192},{64,0},{128,64},{192,128},{1,193},{65,1},{129,65},{193,129... | collective-permute-start | bytes 36872 | tf_op jit(solution)/shard_map/ppermute | solution.py:448
  34.9 0.0 collective-permute-done.1.refs_2_
  34.9 1.1 %collective-permute-done.4.refs_7_ = f32[3,8,128]{2,1,0:T(8,128)S(1)} collective-permute-done((f32[3,8,128]{2,1,0:T(8,128)S(1)}, f32[3,8,128]{2,1,0:T(8,128)S(1)}, u32[]{:S(2)}, u32[]{:S(2)}) %collective-permute-start.4) | collective-permute-done | bytes 12320 | tf_op jit(solution)/shard_map/ppermute | solution.py:448
  36.0 0.0 collective-permute-done.5.refs_8_
  36.0 0.0 collective-permute-done.3.refs_4_
  36.0 0.4 shard_map.98
  36.4 0.3 copy.11
  36.7 14.0 %all_to_all.45 = f32[32,1,2048]{2,1,0:T(1,128)S(1)} all-to-all(f32[32,1,2048]{2,1,0:T(1,128)S(1)} %copy.11), channel_id=1, replica_groups=mesh['cable'=4,'fx'=32,'fz'=2] {'fx'}, dimensions={0} | all-to-all | bytes 524288 | tf_op jit(solution)/shard_map/all_to_all | solution.py:452
  50.8 0.1 copy.20
  50.9 3.8 %collective-permute-start.6 = (f32[32,768]{1,0:T(8,128)S(1)}, f32[32,768]{1,0:T(8,128)S(1)}, u32[]{:S(2)}, u32[]{:S(2)}) collective-permute-start(f32[32,768]{1,0:T(8,128)S(1)} %slice.4), channel_id=1, source_target_pairs={{0,1},{1,0},{2,3},{3,2},{4,5},{5,4},{6,7},{7,6},{8,9},{9,8},{10,11... | collective-permute-start | bytes 294920 | tf_op jit(solution)/shard_map/ppermute | solution.py:448
  54.7 0.4 shard_map.99
  55.1 0.6 collective-permute-done.6.refs_2_
  55.6 0.7 shard_map.100
  56.3 0.4 collective-permute-start.7
  56.8 1.3 %collective-permute-start.8 = (f32[3,8,128]{2,1,0:T(8,128)S(1)}, f32[3,8,128]{2,1,0:T(8,128)S(1)}, u32[]{:S(2)}, u32[]{:S(2)}) collective-permute-start(f32[3,8,128]{2,1,0:T(8,128)S(1)} %get-tuple-element.65), channel_id=1, source_target_pairs={{0,64},{64,128},{128,192},{192,0},{1,65},{65,129},{129,193},{193,1... | collective-permute-start | bytes 36872 | tf_op jit(solution)/shard_map/ppermute | solution.py:448
  58.1 1.4 %collective-permute-start.9 = (f32[3,8,128]{2,1,0:T(8,128)S(1)}, f32[3,8,128]{2,1,0:T(8,128)S(1)}, u32[]{:S(2)}, u32[]{:S(2)}) collective-permute-start(f32[3,8,128]{2,1,0:T(8,128)S(1)} %get-tuple-element.66), channel_id=1, source_target_pairs={{0,192},{64,0},{128,64},{192,128},{1,193},{65,1},{129,65},{193,129... | collective-permute-start | bytes 36872 | tf_op jit(solution)/shard_map/ppermute | solution.py:448
  59.5 1.1 %collective-permute-done.8.refs_7_ = f32[3,8,128]{2,1,0:T(8,128)S(1)} collective-permute-done((f32[3,8,128]{2,1,0:T(8,128)S(1)}, f32[3,8,128]{2,1,0:T(8,128)S(1)}, u32[]{:S(2)}, u32[]{:S(2)}) %collective-permute-start.8) | collective-permute-done | bytes 12320 | tf_op jit(solution)/shard_map/ppermute | solution.py:448
  60.6 0.3 collective-permute-done.9.refs_8_
  60.9 0.0 collective-permute-done.7.refs_4_
  60.9 0.4 shard_map.101
  61.4 0.1 copy.12
  61.5 12.3 %all_to_all.46 = f32[32,1,896]{2,1,0:T(1,128)S(1)} all-to-all(f32[32,1,896]{2,1,0:T(1,128)S(1)} %copy.12), channel_id=1, replica_groups=mesh['cable'=4,'fx'=32,'fz'=2] {'fx'}, dimensions={0} | all-to-all | bytes 229376 | tf_op jit(solution)/shard_map/all_to_all | solution.py:452
  73.8 3.0 %collective-permute-start.10 = (f32[32,896]{1,0:T(8,128)S(1)}, f32[32,896]{1,0:T(8,128)S(1)}, u32[]{:S(2)}, u32[]{:S(2)}) collective-permute-start(f32[32,896]{1,0:T(8,128)S(1)} %bitcast.34), channel_id=1, source_target_pairs={{0,1},{1,0},{2,3},{3,2},{4,5},{5,4},{6,7},{7,6},{8,9},{9,8},{10,11... | collective-permute-start | bytes 344072 | tf_op jit(solution)/shard_map/ppermute | solution.py:448
  76.8 0.8 shard_map.102
  77.6 0.2 collective-permute-done.10.refs_2_
  77.8 0.9 shard_map.103
  78.7 0.4 collective-permute-start.11
  79.2 1.3 %collective-permute-start.12 = (f32[7,8,128]{2,1,0:T(8,128)S(1)}, f32[7,8,128]{2,1,0:T(8,128)S(1)}, u32[]{:S(2)}, u32[]{:S(2)}) collective-permute-start(f32[7,8,128]{2,1,0:T(8,128)S(1)} %get-tuple-element.75), channel_id=1, source_target_pairs={{0,64},{64,128},{128,192},{192,0},{1,65},{65,129},{129,193},{193,1... | collective-permute-start | bytes 86024 | tf_op jit(solution)/shard_map/ppermute | solution.py:448
  80.5 1.4 %collective-permute-start.13 = (f32[7,8,128]{2,1,0:T(8,128)S(1)}, f32[7,8,128]{2,1,0:T(8,128)S(1)}, u32[]{:S(2)}, u32[]{:S(2)}) collective-permute-start(f32[7,8,128]{2,1,0:T(8,128)S(1)} %get-tuple-element.76), channel_id=1, source_target_pairs={{0,192},{64,0},{128,64},{192,128},{1,193},{65,1},{129,65},{193,129... | collective-permute-start | bytes 86024 | tf_op jit(solution)/shard_map/ppermute | solution.py:448
  81.9 1.4 %collective-permute-start.14 = (f32[8,128]{1,0:T(8,128)S(1)}, f32[8,128]{1,0:T(8,128)S(1)}, u32[]{:S(2)}, u32[]{:S(2)}) collective-permute-start(f32[8,128]{1,0:T(8,128)S(1)} %get-tuple-element.78.refs_12_), channel_id=1, source_target_pairs={{0,128},{64,192},{128,0},{192,64},{1,129},{65,193},{129,1},{193,65... | collective-permute-start | bytes 12296 | tf_op jit(solution)/shard_map/ppermute | solution.py:448
  83.3 2.6 %collective-permute-done.14.refs_13_ = f32[8,128]{1,0:T(8,128)S(1)} collective-permute-done((f32[8,128]{1,0:T(8,128)S(1)}, f32[8,128]{1,0:T(8,128)S(1)}, u32[]{:S(2)}, u32[]{:S(2)}) %collective-permute-start.14) | collective-permute-done | bytes 4128 | tf_op jit(solution)/shard_map/ppermute | solution.py:448
  85.8 0.0 collective-permute-done.12.refs_7_
  85.8 1.0 shard_map.104
  86.9 19.5 %all_to_all.47 = f32[256,1,128]{2,1,0:T(1,128)S(1)} all-to-all(f32[256,1,128]{2,1,0:T(1,128)S(1)} %bitcast.38), channel_id=1, replica_groups=mesh['cable'=4,'fx'=32,'fz'=2] {'cable','fx','fz'}, dimensions={0} | all-to-all | bytes 262144 | tf_op jit(solution)/shard_map/all_to_all | solution.py:452
  106.4 0.8 shard_map.105
  (9 shorter events, 0.0 us)
Async XLA Ops:
  2.2 23.8 %copy-start = (f32[3,8,16,128]{3,2,1,0:T(8,128)S(1)}, f32[3,8,16,128]{3,2,1,0:T(8,128)}, u32[]{:S(2)}) copy-start(f32[3,8,16,128]{3,2,1,0:T(8,128)} %param.8) | copy-start | bytes 589828
  2.9 23.1 %all-to-all-start = ((f32[64,1,256]{2,1,0:T(1,128)}), f32[64,1,256]{2,1,0:T(1,128)S(1)}, u32[]{:S(2)}, u32[]{:S(2)}) async-start(f32[64,1,256]{2,1,0:T(1,128)} %copy.10), calls=%async_computation | async-start | bytes 131072 | tf_op jit(solution)/shard_map/all_to_all | solution.py:452
  16.5 9.5 %collective-permute-start.2 = (f32[32,640]{1,0:T(8,128)S(1)}, f32[32,640]{1,0:T(8,128)S(1)}, u32[]{:S(2)}, u32[]{:S(2)}) collective-permute-start(f32[32,640]{1,0:T(8,128)S(1)} %get-tuple-element.47), channel_id=1, source_target_pairs={{0,1},{1,0},{2,3},{3,2},{4,5},{5,4},{6,7},{7,6},{8,9},{9,8},{10,11... | collective-permute-start | bytes 245768 | tf_op jit(solution)/shard_map/ppermute | solution.py:448
  26.0 10.1 %copy-start.1 = (f32[8,16,128]{2,1,0:T(8,128)S(1)}, f32[8,16,128]{2,1,0:T(8,128)}, u32[]{:S(2)}) copy-start(f32[8,16,128]{2,1,0:T(8,128)} %param.9) | copy-start | bytes 196612
  27.0 9.0 %collective-permute-start.3 = (f32[3,128,128]{2,1,0:T(8,128)S(1)}, f32[3,128,128]{2,1,0:T(8,128)S(1)}, u32[]{:S(2)}, u32[]{:S(2)}) collective-permute-start(f32[3,128,128]{2,1,0:T(8,128)S(1)} %get-tuple-element.49.refs_3_), channel_id=1, source_target_pairs={{0,1},{1,0},{2,3},{3,2},{4,5},{5,4},{6,7},{7,6},{8,9},{9,8},{10,11... | collective-permute-start | bytes 589832 | tf_op jit(solution)/shard_map/ppermute | solution.py:448
  27.4 7.5 %collective-permute-start = (f32[3,16,128]{2,1,0:T(8,128)S(1)}, f32[3,16,128]{2,1,0:T(8,128)S(1)}, u32[]{:S(2)}, u32[]{:S(2)}) collective-permute-start(f32[3,16,128]{2,1,0:T(8,128)S(1)} %get-tuple-element.42), channel_id=1, source_target_pairs={{0,2},{2,4},{4,6},{6,8},{8,10},{10,12},{12,14},{14,16},{16,18},{18... | collective-permute-start | bytes 73736 | tf_op jit(solution)/shard_map/ppermute | solution.py:448
  27.6 7.3 %collective-permute-start.1 = (f32[3,16,128]{2,1,0:T(8,128)S(1)}, f32[3,16,128]{2,1,0:T(8,128)S(1)}, u32[]{:S(2)}, u32[]{:S(2)}) collective-permute-start(f32[3,16,128]{2,1,0:T(8,128)S(1)} %get-tuple-element.43), channel_id=1, source_target_pairs={{0,62},{2,0},{4,2},{6,4},{8,6},{10,8},{12,10},{14,12},{16,14},{18,... | collective-permute-start | bytes 73736 | tf_op jit(solution)/shard_map/ppermute | solution.py:448
  32.2 3.8 %collective-permute-start.4 = (f32[3,8,128]{2,1,0:T(8,128)S(1)}, f32[3,8,128]{2,1,0:T(8,128)S(1)}, u32[]{:S(2)}, u32[]{:S(2)}) collective-permute-start(f32[3,8,128]{2,1,0:T(8,128)S(1)} %get-tuple-element.52), channel_id=1, source_target_pairs={{0,64},{64,128},{128,192},{192,0},{1,65},{65,129},{129,193},{193,1... | collective-permute-start | bytes 36872 | tf_op jit(solution)/shard_map/ppermute | solution.py:448
  33.5 2.5 %collective-permute-start.5 = (f32[3,8,128]{2,1,0:T(8,128)S(1)}, f32[3,8,128]{2,1,0:T(8,128)S(1)}, u32[]{:S(2)}, u32[]{:S(2)}) collective-permute-start(f32[3,8,128]{2,1,0:T(8,128)S(1)} %get-tuple-element.53), channel_id=1, source_target_pairs={{0,192},{64,0},{128,64},{192,128},{1,193},{65,1},{129,65},{193,129... | collective-permute-start | bytes 36872 | tf_op jit(solution)/shard_map/ppermute | solution.py:448
  50.9 4.8 %collective-permute-start.6 = (f32[32,768]{1,0:T(8,128)S(1)}, f32[32,768]{1,0:T(8,128)S(1)}, u32[]{:S(2)}, u32[]{:S(2)}) collective-permute-start(f32[32,768]{1,0:T(8,128)S(1)} %slice.4), channel_id=1, source_target_pairs={{0,1},{1,0},{2,3},{3,2},{4,5},{5,4},{6,7},{7,6},{8,9},{9,8},{10,11... | collective-permute-start | bytes 294920 | tf_op jit(solution)/shard_map/ppermute | solution.py:448
  56.3 4.6 %collective-permute-start.7 = (f32[3,128,128]{2,1,0:T(8,128)S(1)}, f32[3,128,128]{2,1,0:T(8,128)S(1)}, u32[]{:S(2)}, u32[]{:S(2)}) collective-permute-start(f32[3,128,128]{2,1,0:T(8,128)S(1)} %get-tuple-element.62.refs_3_), channel_id=1, source_target_pairs={{0,1},{1,0},{2,3},{3,2},{4,5},{5,4},{6,7},{7,6},{8,9},{9,8},{10,11... | collective-permute-start | bytes 589832 | tf_op jit(solution)/shard_map/ppermute | solution.py:448
  56.8 3.8 %collective-permute-start.8 = (f32[3,8,128]{2,1,0:T(8,128)S(1)}, f32[3,8,128]{2,1,0:T(8,128)S(1)}, u32[]{:S(2)}, u32[]{:S(2)}) collective-permute-start(f32[3,8,128]{2,1,0:T(8,128)S(1)} %get-tuple-element.65), channel_id=1, source_target_pairs={{0,64},{64,128},{128,192},{192,0},{1,65},{65,129},{129,193},{193,1... | collective-permute-start | bytes 36872 | tf_op jit(solution)/shard_map/ppermute | solution.py:448
  58.1 2.8 %collective-permute-start.9 = (f32[3,8,128]{2,1,0:T(8,128)S(1)}, f32[3,8,128]{2,1,0:T(8,128)S(1)}, u32[]{:S(2)}, u32[]{:S(2)}) collective-permute-start(f32[3,8,128]{2,1,0:T(8,128)S(1)} %get-tuple-element.66), channel_id=1, source_target_pairs={{0,192},{64,0},{128,64},{192,128},{1,193},{65,1},{129,65},{193,129... | collective-permute-start | bytes 36872 | tf_op jit(solution)/shard_map/ppermute | solution.py:448
  73.8 4.0 %collective-permute-start.10 = (f32[32,896]{1,0:T(8,128)S(1)}, f32[32,896]{1,0:T(8,128)S(1)}, u32[]{:S(2)}, u32[]{:S(2)}) collective-permute-start(f32[32,896]{1,0:T(8,128)S(1)} %bitcast.34), channel_id=1, source_target_pairs={{0,1},{1,0},{2,3},{3,2},{4,5},{5,4},{6,7},{7,6},{8,9},{9,8},{10,11... | collective-permute-start | bytes 344072 | tf_op jit(solution)/shard_map/ppermute | solution.py:448
  78.7 7.1 %collective-permute-start.11 = (f32[6,128,128]{2,1,0:T(8,128)S(1)}, f32[6,128,128]{2,1,0:T(8,128)S(1)}, u32[]{:S(2)}, u32[]{:S(2)}) collective-permute-start(f32[6,128,128]{2,1,0:T(8,128)S(1)} %get-tuple-element.72.refs_3_), channel_id=1, source_target_pairs={{0,1},{1,0},{2,3},{3,2},{4,5},{5,4},{6,7},{7,6},{8,9},{9,8},{10,11... | collective-permute-start | bytes 1179656 | tf_op jit(solution)/shard_map/ppermute | solution.py:448
  79.2 6.6 %collective-permute-start.12 = (f32[7,8,128]{2,1,0:T(8,128)S(1)}, f32[7,8,128]{2,1,0:T(8,128)S(1)}, u32[]{:S(2)}, u32[]{:S(2)}) collective-permute-start(f32[7,8,128]{2,1,0:T(8,128)S(1)} %get-tuple-element.75), channel_id=1, source_target_pairs={{0,64},{64,128},{128,192},{192,0},{1,65},{65,129},{129,193},{193,1... | collective-permute-start | bytes 86024 | tf_op jit(solution)/shard_map/ppermute | solution.py:448
  80.5 5.4 %collective-permute-start.13 = (f32[7,8,128]{2,1,0:T(8,128)S(1)}, f32[7,8,128]{2,1,0:T(8,128)S(1)}, u32[]{:S(2)}, u32[]{:S(2)}) collective-permute-start(f32[7,8,128]{2,1,0:T(8,128)S(1)} %get-tuple-element.76), channel_id=1, source_target_pairs={{0,192},{64,0},{128,64},{192,128},{1,193},{65,1},{129,65},{193,129... | collective-permute-start | bytes 86024 | tf_op jit(solution)/shard_map/ppermute | solution.py:448
  81.9 4.0 %collective-permute-start.14 = (f32[8,128]{1,0:T(8,128)S(1)}, f32[8,128]{1,0:T(8,128)S(1)}, u32[]{:S(2)}, u32[]{:S(2)}) collective-permute-start(f32[8,128]{1,0:T(8,128)S(1)} %get-tuple-element.78.refs_12_), channel_id=1, source_target_pairs={{0,128},{64,192},{128,0},{192,64},{1,129},{65,193},{129,1},{193,65... | collective-permute-start | bytes 12296 | tf_op jit(solution)/shard_map/ppermute | solution.py:448
where the time goes:
time: 107 us
  blocking collectives  45.8 us (43%)
  starting transfers between devices  36 us (34%)
  waiting for transfers between devices  14.8 us (14%)
  Pallas kernels  8.58 us (8%)
  local copies, waits for them, and re-layouts  1.21 us (1%)
    all_to_all x3, blocking collectives, exchange(): return lax.all_to_all(array, axes, 0, 0, tiled=True)  45.8 us
    ppermute x15, starting transfers between devices, shifted(): lax.ppermute(array, axis, [(i, (i + by) % count) for i in range(count)])  23 us
    all_to_all x1, starting transfers between devices, exchange(): return lax.all_to_all(array, axes, 0, 0, tiled=True)  13 us
    all_to_all x1, waiting for transfers between devices, exchange(): return lax.all_to_all(array, axes, 0, 0, tiled=True)  8.92 us
    pallas_call x11, Pallas kernels, call(): pl.pallas_call(kernel, out_shape=outs, in_specs=[pl.BlockSpec(memory_spac...  8.58 us
    ppermute x15, waiting for transfers between devices, shifted(): lax.ppermute(array, axis, [(i, (i + by) % count) for i in range(count)])  5.85 us
  transfers between devices with their start and end apart: 16, of which 7 were waited for; matrix products, arithmetic and copies ran while one was open for 0% of the time, Pallas kernels for 2%

commit v1 on v0

--- a/solution.py
+++ b/solution.py
@@ -209,10 +209,10 @@
     return [rows[R_REST + c : R_REST + c + 1] + cr * sampled[c] for c in range(3)]
 
 
-def prepare_kernel(t, *refs):
+def prepare_kernel(t, sets, *refs):
     static, sent, (wxy_out, wz_out, plane_out, slots, turned) = refs[0], refs[1:-5], refs[-5:]
     turn_static(static, turned, t)
-    for j in range(SETS):
+    for j in sets:
         rows = slot_rows(turned, t, j)
         wxy, wz = tables(rows, (None, SX - 1, 0)[j])
         hi, low = split(wz)
@@ -252,27 +252,25 @@
     if t == 0:
         static, velocity = refs[0:2]
         sent = ()
-        field, xl, xu, ylo, yhi, *tabled, turned = refs[2:]
-        prepare_kernel(0, static, *tabled, turned)
+        field, ylo, yhi, *tabled, turned = refs[2:]
+        prepare_kernel(0, (0,), static, *tabled, turned)
     else:
         velocity, sent, tabled = refs[0], refs[1:3], refs[3:7]
-        field, xl, xu, ylo, yhi, aux = refs[7:13]
+        field, ylo, yhi, aux = refs[7:11]
         aux[...] = jnp.zeros_like(aux)
-    wxy, wz, plane, slots = tabled
-    for j, out in enumerate((field, xl, xu)):
-        rows = slots[32 * j : 32 * j + 32, :]
-        bases, kept = displacements(t, rows, sent)
-        height = SY if j else XY
-        for n, base in enumerate(bases):
-            forced = spread(plane[j - 1] if j else wxy[...], wz[j], base)
+    wxy, wz, _, slots = tabled
+    rows = slots[0:32, :]
+    bases, kept = displacements(t, rows, sent)
+    for n, base in enumerate(bases):
+        forced = spread(wxy[...], wz[0], base)
+        for c in range(3):
+            part = forced[XY * c : XY * (c + 1)]
+            field[3 * n + c] = part + velocity[c] if n == 0 else part
+    if t > 0:
+        for n, group in enumerate(kept):
             for c in range(3):
-                part = forced[height * c : height * (c + 1)]
-                out[3 * n + c] = part + velocity[c] if n == 0 and j == 0 else part
-        if j == 0 and t > 0:
-            for n, group in enumerate(kept):
-                for c in range(3):
-                    aux[3 * n + c : 3 * n + c + 1, :] = group[c]
-            aux[16:20, :] = rows[R_REST : R_REST + 4]
+                aux[3 * n + c : 3 * n + c + 1, :] = group[c]
+        aux[16:20, :] = rows[R_REST : R_REST + 4]
     for n in range(3 * len(bases)):
         ylo[n] = field[n, pl.ds(0, SX, stride=SY), :]
         yhi[n] = field[n, pl.ds(SY - 1, SX, stride=SY), :]
@@ -282,7 +280,23 @@
         total = jnp.broadcast_to(total, (8, 128))
         ylo[6] = total
         yhi[6] = total
-        refs[13][...] = total
+        refs[11][...] = total
+
+
+def sides_kernel(t, *refs):
+    if t == 0:
+        (static, *outs), tabled, turned = refs[0:3], refs[3:7], refs[7]
+        sent = ()
+        prepare_kernel(0, (1, 2), static, *tabled, turned)
+    else:
+        sent, tabled, outs = refs[0:2], refs[2:6], refs[6:8]
+    _, wz, plane, slots = tabled
+    for j, out in enumerate(outs):
+        bases, _ = displacements(t, slots[32 * j + 32 : 32 * j + 64, :], sent)
+        for n, base in enumerate(bases):
+            forced = spread(plane[j], wz[j + 1], base)
+            for c in range(3):
+                out[3 * n + c] = forced[SY * c : SY * (c + 1)]
 
 
 def wake(u, beside_z, xl, xu, yl, yu, viscosity):
@@ -473,7 +487,7 @@
         [shape(HALF, LATE), shape(HALF, LATE), shape(8, SEG_DEV)],
         [pltpu.VMEM((LATE, 128), F32)],
     )
-    static, *carried = lax.optimization_barrier((static, keep, shifted(give, "fz", 1)))
+    carried = (keep, shifted(give, "fz", 1))
     table_outs = [
         shape(XY, SLOTS),
         shape(SETS, 2 * SZ, SLOTS, kind=BF16),
@@ -485,16 +499,23 @@
     for t in range(3):
         n = 6 if t == 2 else 3
         faced = 7 if t == 2 else 3
-        outs = [shape(n, XY, SZ), shape(n, SY, SZ), shape(n, SY, SZ)] + [shape(faced, SX, SZ)] * 2
+        outs = [shape(n, XY, SZ), shape(faced, SX, SZ), shape(faced, SX, SZ)]
+        planes = [shape(n, SY, SZ)] * 2
         kernel = functools.partial(spread_kernel, t)
+        beside = functools.partial(sides_kernel, t)
         if t == 0:
-            field, xl, xu, ylo, yhi, *tabled = call(kernel, (static, flow), outs + table_outs, turned)
+            field, ylo, yhi, *tabled = call(kernel, (static, flow), outs + table_outs, turned)
             extra = []
+            spare = [pltpu.VMEM(a.shape, a.dtype) for a in table_outs]
+            wait_for, ins = (static,), ()
         else:
             outs.append(shape(24, SLOTS))
             if t == 2:
                 outs.append(shape(8, 128))
-            field, xl, xu, ylo, yhi, *extra = call(kernel, (flow, *sent, *tabled), outs)
+            field, ylo, yhi, *extra = call(kernel, (flow, *sent, *tabled), outs)
+            spare = []
+            wait_for, ins = sent, tabled
+        xl, xu = call(beside, (*wait_for, *ins), planes, [*spare, *turned] if t == 0 else ())
         yl = shifted(yhi, "cable", 1)
         yu = shifted(ylo, "cable", -1)
         beside_z = shifted(field, "fz", 1)
@@ -510,7 +531,7 @@
             if t == 0:
                 static, before = half, ()
             sent = (half, shifted(half if t else half[:, : 3 * SLOTS], "fz", 1))
-            tabled = call(functools.partial(prepare_kernel, t + 1), (static, *before), table_outs, turned)
+            tabled = call(functools.partial(prepare_kernel, t + 1, range(SETS)), (static, *before), table_outs, turned)
             before = sent
         else:
             ins.append(across)

time: 107 us -> 107 us (level)
  blocking collectives: 45.8 us -> 68.2 us
  starting transfers between devices: 36 us -> 24.5 us
  waiting for transfers between devices: 14.8 us -> 3.44 us
    all_to_all x3 -> x4, blocking collectives: 45.8 us -> 68.2 us  [exchange(): return lax.all_to_all(array, axes, 0, 0, tiled=True)]
    all_to_all x1 -> x0, starting transfers between devices: 13 us -> none  [exchange(): return lax.all_to_all(array, axes, 0, 0, tiled=True)]
    all_to_all x1 -> x0, waiting for transfers between devices: 8.92 us -> none  [exchange(): return lax.all_to_all(array, axes, 0, 0, tiled=True)]
    ppermute x15, waiting for transfers between devices: 5.85 us -> 3.44 us  [shifted(): lax.ppermute(array, axis, [(i, (i + by) % count) for i in range(count)])]
    ppermute x15, starting transfers between devices: 23 us -> 24.5 us  [shifted(): lax.ppermute(array, axis, [(i, (i + by) % count) for i in range(count)])]
    pallas_call x11 -> x14, Pallas kernels: 8.58 us -> 9.32 us  [call(): pl.pallas_call(kernel, out_shape=outs, in_specs=[pl.BlockSpec(memory_spac...]
  transfers between devices with their start and end apart: 16 -> 15, of which waited for: 7 -> 5; matrix products, arithmetic and copies ran while one was open for 0% -> 0% of each run, Pallas kernels for 2% -> 3%
where the time goes in v1:
time: 107 us
  blocking collectives  68.2 us (64%)
  starting transfers between devices  24.5 us (23%)
  Pallas kernels  9.32 us (9%)
  waiting for transfers between devices  3.44 us (3%)
    all_to_all x4, blocking collectives, exchange(): return lax.all_to_all(array, axes, 0, 0, tiled=True)  68.2 us
    ppermute x15, starting transfers between devices, shifted(): lax.ppermute(array, axis, [(i, (i + by) % count) for i in range(count)])  24.5 us
    pallas_call x14, Pallas kernels, call(): pl.pallas_call(kernel, out_shape=outs, in_specs=[pl.BlockSpec(memory_spac...  9.32 us
    ppermute x15, waiting for transfers between devices, shifted(): lax.ppermute(array, axis, [(i, (i + by) % count) for i in range(count)])  3.44 us
  transfers between devices with their start and end apart: 15, of which 5 were waited for; matrix products, arithmetic and copies ran while one was open for 0% of the time, Pallas kernels for 3%

profile of v1, /device:TPU:1, one launch (start us, length us, event | category | flops | bytes accessed | tf_op | source)
XLA Modules:
  0.0 106.8 jit_solution(5651922087623481442)
XLA Ops:
  0.6 1.5 %shard_map.95 = (f32[64,256]{1,0:T(8,128)S(1)}, f32[56,64]{1,0:T(8,128)S(1)}, f32[24,64]{1,0:T(8,128)}, f32[3,16,128]{2,1,0:T(8,128)S(1)}, f32[3,16,128]{2,1,0:T(8,128)S(1)}) custom-call(f32[3,64]{1,0:T(4,128)} %refs_0_.1, f32[3,64]{1,0:T(4,128)} %refs_1_.1, f32[1,64]{1,0:T(1,128)} %bitcast.43, f32[3,12,64]{2,1,0:T(8,128)} %refs_3_.1, s32[3,64]{1,0:T(4,128)} %refs_4_.1, ...), custom_call_target="tpu_custom_call" | custom-call | bytes 344320 | tf_op jit(solution)/shard_map/pallas_call | solution.py:449
  2.2 0.0 copy-start
  2.2 0.1 copy.10
  2.3 22.9 %all_to_all.44 = f32[64,1,256]{2,1,0:T(1,128)S(1)} all-to-all(f32[64,1,256]{2,1,0:T(1,128)S(1)} %copy.10), channel_id=1, replica_groups=mesh['cable'=4,'fx'=32,'fz'=2] {'fx','fz'}, dimensions={0} | all-to-all | bytes 131072 | tf_op jit(solution)/shard_map/all_to_all | solution.py:466
  25.1 0.8 shard_map.96
  25.9 0.4 collective-permute-start.2
  26.3 0.6 shard_map.98
  27.0 0.2 collective-permute-start.5
  27.2 0.2 collective-permute-start
  27.4 4.6 %collective-permute-start.1 = (f32[3,16,128]{2,1,0:T(8,128)S(1)}, f32[3,16,128]{2,1,0:T(8,128)S(1)}, u32[]{:S(2)}, u32[]{:S(2)}) collective-permute-start(f32[3,16,128]{2,1,0:T(8,128)S(1)} %get-tuple-element.40), channel_id=1, source_target_pairs={{0,62},{2,0},{4,2},{6,4},{8,6},{10,8},{12,10},{14,12},{16,14},{18,... | collective-permute-start | bytes 73736 | tf_op jit(solution)/shard_map/ppermute | solution.py:462
  32.0 1.3 %collective-permute-start.3 = (f32[3,8,128]{2,1,0:T(8,128)S(1)}, f32[3,8,128]{2,1,0:T(8,128)S(1)}, u32[]{:S(2)}, u32[]{:S(2)}) collective-permute-start(f32[3,8,128]{2,1,0:T(8,128)S(1)} %get-tuple-element.45), channel_id=1, source_target_pairs={{0,64},{64,128},{128,192},{192,0},{1,65},{65,129},{129,193},{193,1... | collective-permute-start | bytes 36872 | tf_op jit(solution)/shard_map/ppermute | solution.py:462
  33.3 2.6 %collective-permute-start.4 = (f32[3,8,128]{2,1,0:T(8,128)S(1)}, f32[3,8,128]{2,1,0:T(8,128)S(1)}, u32[]{:S(2)}, u32[]{:S(2)}) collective-permute-start(f32[3,8,128]{2,1,0:T(8,128)S(1)} %get-tuple-element.46), channel_id=1, source_target_pairs={{0,192},{64,0},{128,64},{192,128},{1,193},{65,1},{129,65},{193,129... | collective-permute-start | bytes 36872 | tf_op jit(solution)/shard_map/ppermute | solution.py:462
  35.9 0.5 shard_map.97
  36.4 0.0 collective-permute-done.5.refs_12_
  36.4 0.0 collective-permute-done.3.refs_7_
  36.4 0.3 collective-permute-done.4.refs_8_
  36.7 0.0 collective-permute-done.2.refs_4_
  36.7 0.4 shard_map.99
  37.1 0.3 copy.11
  37.4 13.6 %all_to_all.45 = f32[32,1,2048]{2,1,0:T(1,128)S(1)} all-to-all(f32[32,1,2048]{2,1,0:T(1,128)S(1)} %copy.11), channel_id=1, replica_groups=mesh['cable'=4,'fx'=32,'fz'=2] {'fx'}, dimensions={0} | all-to-all | bytes 524288 | tf_op jit(solution)/shard_map/all_to_all | solution.py:466
  51.0 0.1 copy.20
  51.1 3.7 %collective-permute-start.6 = (f32[32,768]{1,0:T(8,128)S(1)}, f32[32,768]{1,0:T(8,128)S(1)}, u32[]{:S(2)}, u32[]{:S(2)}) collective-permute-start(f32[32,768]{1,0:T(8,128)S(1)} %slice.4), channel_id=1, source_target_pairs={{0,1},{1,0},{2,3},{3,2},{4,5},{5,4},{6,7},{7,6},{8,9},{9,8},{10,11... | collective-permute-start | bytes 294920 | tf_op jit(solution)/shard_map/ppermute | solution.py:462
  54.7 0.4 shard_map.100
  55.1 0.6 collective-permute-done.6.refs_2_.refs_1_
  55.7 0.5 shard_map.101
  56.1 0.4 collective-permute-start.7
  56.6 1.0 collective-permute-start.8
  57.6 2.2 %collective-permute-start.9 = (f32[3,8,128]{2,1,0:T(8,128)S(1)}, f32[3,8,128]{2,1,0:T(8,128)S(1)}, u32[]{:S(2)}, u32[]{:S(2)}) collective-permute-start(f32[3,8,128]{2,1,0:T(8,128)S(1)} %get-tuple-element.60), channel_id=1, source_target_pairs={{0,192},{64,0},{128,64},{192,128},{1,193},{65,1},{129,65},{193,129... | collective-permute-start | bytes 36872 | tf_op jit(solution)/shard_map/ppermute | solution.py:462
  59.8 0.5 shard_map.102
  60.3 0.6 collective-permute-done.8.refs_7_
  60.9 0.0 collective-permute-done.9.refs_8_
  60.9 0.0 collective-permute-done.7.refs_4_
  60.9 0.5 shard_map.103
  61.4 0.1 copy.12
  61.5 12.3 %all_to_all.46 = f32[32,1,896]{2,1,0:T(1,128)S(1)} all-to-all(f32[32,1,896]{2,1,0:T(1,128)S(1)} %copy.12), channel_id=1, replica_groups=mesh['cable'=4,'fx'=32,'fz'=2] {'fx'}, dimensions={0} | all-to-all | bytes 229376 | tf_op jit(solution)/shard_map/all_to_all | solution.py:466
  73.8 2.8 %collective-permute-start.10 = (f32[32,896]{1,0:T(8,128)S(1)}, f32[32,896]{1,0:T(8,128)S(1)}, u32[]{:S(2)}, u32[]{:S(2)}) collective-permute-start(f32[32,896]{1,0:T(8,128)S(1)} %bitcast.31), channel_id=1, source_target_pairs={{0,1},{1,0},{2,3},{3,2},{4,5},{5,4},{6,7},{7,6},{8,9},{9,8},{10,11... | collective-permute-start | bytes 344072 | tf_op jit(solution)/shard_map/ppermute | solution.py:462
  76.5 0.8 shard_map.104
  77.3 0.2 collective-permute-done.10.refs_2_.refs_1_
  77.5 0.6 shard_map.105
  78.1 0.4 collective-permute-start.11
  78.5 1.2 %collective-permute-start.12 = (f32[7,8,128]{2,1,0:T(8,128)S(1)}, f32[7,8,128]{2,1,0:T(8,128)S(1)}, u32[]{:S(2)}, u32[]{:S(2)}) collective-permute-start(f32[7,8,128]{2,1,0:T(8,128)S(1)} %get-tuple-element.69), channel_id=1, source_target_pairs={{0,64},{64,128},{128,192},{192,0},{1,65},{65,129},{129,193},{193,1... | collective-permute-start | bytes 86024 | tf_op jit(solution)/shard_map/ppermute | solution.py:462
  79.7 1.8 %collective-permute-start.13 = (f32[7,8,128]{2,1,0:T(8,128)S(1)}, f32[7,8,128]{2,1,0:T(8,128)S(1)}, u32[]{:S(2)}, u32[]{:S(2)}) collective-permute-start(f32[7,8,128]{2,1,0:T(8,128)S(1)} %get-tuple-element.70), channel_id=1, source_target_pairs={{0,192},{64,0},{128,64},{192,128},{1,193},{65,1},{129,65},{193,129... | collective-permute-start | bytes 86024 | tf_op jit(solution)/shard_map/ppermute | solution.py:462
  81.5 1.7 %collective-permute-start.14 = (f32[8,128]{1,0:T(8,128)S(1)}, f32[8,128]{1,0:T(8,128)S(1)}, u32[]{:S(2)}, u32[]{:S(2)}) collective-permute-start(f32[8,128]{1,0:T(8,128)S(1)} %get-tuple-element.72.refs_12_), channel_id=1, source_target_pairs={{0,128},{64,192},{128,0},{192,64},{1,129},{65,193},{129,1},{193,65... | collective-permute-start | bytes 12296 | tf_op jit(solution)/shard_map/ppermute | solution.py:462
  83.2 0.5 shard_map.106
  83.7 1.7 %collective-permute-done.14.refs_13_ = f32[8,128]{1,0:T(8,128)S(1)} collective-permute-done((f32[8,128]{1,0:T(8,128)S(1)}, f32[8,128]{1,0:T(8,128)S(1)}, u32[]{:S(2)}, u32[]{:S(2)}) %collective-permute-start.14) | collective-permute-done | bytes 4128 | tf_op jit(solution)/shard_map/ppermute | solution.py:462
  85.5 1.0 shard_map.107
  86.5 19.5 %all_to_all.47 = f32[256,1,128]{2,1,0:T(1,128)S(1)} all-to-all(f32[256,1,128]{2,1,0:T(1,128)S(1)} %bitcast.41), channel_id=1, replica_groups=mesh['cable'=4,'fx'=32,'fz'=2] {'cable','fx','fz'}, dimensions={0} | all-to-all | bytes 262144 | tf_op jit(solution)/shard_map/all_to_all | solution.py:466
  106.0 0.8 shard_map.108
  (11 shorter events, 0.0 us)
Async XLA Ops:
  2.2 23.0 %copy-start = (f32[3,8,16,128]{3,2,1,0:T(8,128)S(1)}, f32[3,8,16,128]{3,2,1,0:T(8,128)}, u32[]{:S(2)}) copy-start(f32[3,8,16,128]{3,2,1,0:T(8,128)} %param.8) | copy-start | bytes 589828
  25.9 10.8 %copy-start.1 = (f32[8,16,128]{2,1,0:T(8,128)S(1)}, f32[8,16,128]{2,1,0:T(8,128)}, u32[]{:S(2)}) copy-start(f32[8,16,128]{2,1,0:T(8,128)} %param.9) | copy-start | bytes 196612
  25.9 10.8 %collective-permute-start.2 = (f32[3,128,128]{2,1,0:T(8,128)S(1)}, f32[3,128,128]{2,1,0:T(8,128)S(1)}, u32[]{:S(2)}, u32[]{:S(2)}) collective-permute-start(f32[3,128,128]{2,1,0:T(8,128)S(1)} %get-tuple-element.42.refs_3_), channel_id=1, source_target_pairs={{0,1},{1,0},{2,3},{3,2},{4,5},{5,4},{6,7},{7,6},{8,9},{9,8},{10,11... | collective-permute-start | bytes 589832 | tf_op jit(solution)/shard_map/ppermute | solution.py:462
  27.0 9.5 %collective-permute-start.5 = (f32[32,640]{1,0:T(8,128)S(1)}, f32[32,640]{1,0:T(8,128)S(1)}, u32[]{:S(2)}, u32[]{:S(2)}) collective-permute-start(f32[32,640]{1,0:T(8,128)S(1)} %get-tuple-element.51), channel_id=1, source_target_pairs={{0,1},{1,0},{2,3},{3,2},{4,5},{5,4},{6,7},{7,6},{8,9},{9,8},{10,11... | collective-permute-start | bytes 245768 | tf_op jit(solution)/shard_map/ppermute | solution.py:462
  27.2 6.1 %collective-permute-start = (f32[3,16,128]{2,1,0:T(8,128)S(1)}, f32[3,16,128]{2,1,0:T(8,128)S(1)}, u32[]{:S(2)}, u32[]{:S(2)}) collective-permute-start(f32[3,16,128]{2,1,0:T(8,128)S(1)} %get-tuple-element.39), channel_id=1, source_target_pairs={{0,2},{2,4},{4,6},{6,8},{8,10},{10,12},{12,14},{14,16},{16,18},{18... | collective-permute-start | bytes 73736 | tf_op jit(solution)/shard_map/ppermute | solution.py:462
  27.4 9.1 %collective-permute-start.1 = (f32[3,16,128]{2,1,0:T(8,128)S(1)}, f32[3,16,128]{2,1,0:T(8,128)S(1)}, u32[]{:S(2)}, u32[]{:S(2)}) collective-permute-start(f32[3,16,128]{2,1,0:T(8,128)S(1)} %get-tuple-element.40), channel_id=1, source_target_pairs={{0,62},{2,0},{4,2},{6,4},{8,6},{10,8},{12,10},{14,12},{16,14},{18,... | collective-permute-start | bytes 73736 | tf_op jit(solution)/shard_map/ppermute | solution.py:462
  32.0 4.5 %collective-permute-start.3 = (f32[3,8,128]{2,1,0:T(8,128)S(1)}, f32[3,8,128]{2,1,0:T(8,128)S(1)}, u32[]{:S(2)}, u32[]{:S(2)}) collective-permute-start(f32[3,8,128]{2,1,0:T(8,128)S(1)} %get-tuple-element.45), channel_id=1, source_target_pairs={{0,64},{64,128},{128,192},{192,0},{1,65},{65,129},{129,193},{193,1... | collective-permute-start | bytes 36872 | tf_op jit(solution)/shard_map/ppermute | solution.py:462
  33.3 3.5 %collective-permute-start.4 = (f32[3,8,128]{2,1,0:T(8,128)S(1)}, f32[3,8,128]{2,1,0:T(8,128)S(1)}, u32[]{:S(2)}, u32[]{:S(2)}) collective-permute-start(f32[3,8,128]{2,1,0:T(8,128)S(1)} %get-tuple-element.46), channel_id=1, source_target_pairs={{0,192},{64,0},{128,64},{192,128},{1,193},{65,1},{129,65},{193,129... | collective-permute-start | bytes 36872 | tf_op jit(solution)/shard_map/ppermute | solution.py:462
  51.1 4.6 %collective-permute-start.6 = (f32[32,768]{1,0:T(8,128)S(1)}, f32[32,768]{1,0:T(8,128)S(1)}, u32[]{:S(2)}, u32[]{:S(2)}) collective-permute-start(f32[32,768]{1,0:T(8,128)S(1)} %slice.4), channel_id=1, source_target_pairs={{0,1},{1,0},{2,3},{3,2},{4,5},{5,4},{6,7},{7,6},{8,9},{9,8},{10,11... | collective-permute-start | bytes 294920 | tf_op jit(solution)/shard_map/ppermute | solution.py:462
  56.1 4.8 %collective-permute-start.7 = (f32[3,128,128]{2,1,0:T(8,128)S(1)}, f32[3,128,128]{2,1,0:T(8,128)S(1)}, u32[]{:S(2)}, u32[]{:S(2)}) collective-permute-start(f32[3,128,128]{2,1,0:T(8,128)S(1)} %get-tuple-element.56.refs_3_), channel_id=1, source_target_pairs={{0,1},{1,0},{2,3},{3,2},{4,5},{5,4},{6,7},{7,6},{8,9},{9,8},{10,11... | collective-permute-start | bytes 589832 | tf_op jit(solution)/shard_map/ppermute | solution.py:462
  56.6 4.3 %collective-permute-start.8 = (f32[3,8,128]{2,1,0:T(8,128)S(1)}, f32[3,8,128]{2,1,0:T(8,128)S(1)}, u32[]{:S(2)}, u32[]{:S(2)}) collective-permute-start(f32[3,8,128]{2,1,0:T(8,128)S(1)} %get-tuple-element.59), channel_id=1, source_target_pairs={{0,64},{64,128},{128,192},{192,0},{1,65},{65,129},{129,193},{193,1... | collective-permute-start | bytes 36872 | tf_op jit(solution)/shard_map/ppermute | solution.py:462
  57.6 3.3 %collective-permute-start.9 = (f32[3,8,128]{2,1,0:T(8,128)S(1)}, f32[3,8,128]{2,1,0:T(8,128)S(1)}, u32[]{:S(2)}, u32[]{:S(2)}) collective-permute-start(f32[3,8,128]{2,1,0:T(8,128)S(1)} %get-tuple-element.60), channel_id=1, source_target_pairs={{0,192},{64,0},{128,64},{192,128},{1,193},{65,1},{129,65},{193,129... | collective-permute-start | bytes 36872 | tf_op jit(solution)/shard_map/ppermute | solution.py:462
  73.8 3.7 %collective-permute-start.10 = (f32[32,896]{1,0:T(8,128)S(1)}, f32[32,896]{1,0:T(8,128)S(1)}, u32[]{:S(2)}, u32[]{:S(2)}) collective-permute-start(f32[32,896]{1,0:T(8,128)S(1)} %bitcast.31), channel_id=1, source_target_pairs={{0,1},{1,0},{2,3},{3,2},{4,5},{5,4},{6,7},{7,6},{8,9},{9,8},{10,11... | collective-permute-start | bytes 344072 | tf_op jit(solution)/shard_map/ppermute | solution.py:462
  78.1 7.4 %collective-permute-start.11 = (f32[6,128,128]{2,1,0:T(8,128)S(1)}, f32[6,128,128]{2,1,0:T(8,128)S(1)}, u32[]{:S(2)}, u32[]{:S(2)}) collective-permute-start(f32[6,128,128]{2,1,0:T(8,128)S(1)} %get-tuple-element.66.refs_3_), channel_id=1, source_target_pairs={{0,1},{1,0},{2,3},{3,2},{4,5},{5,4},{6,7},{7,6},{8,9},{9,8},{10,11... | collective-permute-start | bytes 1179656 | tf_op jit(solution)/shard_map/ppermute | solution.py:462
  78.5 7.0 %collective-permute-start.12 = (f32[7,8,128]{2,1,0:T(8,128)S(1)}, f32[7,8,128]{2,1,0:T(8,128)S(1)}, u32[]{:S(2)}, u32[]{:S(2)}) collective-permute-start(f32[7,8,128]{2,1,0:T(8,128)S(1)} %get-tuple-element.69), channel_id=1, source_target_pairs={{0,64},{64,128},{128,192},{192,0},{1,65},{65,129},{129,193},{193,1... | collective-permute-start | bytes 86024 | tf_op jit(solution)/shard_map/ppermute | solution.py:462
  79.7 5.8 %collective-permute-start.13 = (f32[7,8,128]{2,1,0:T(8,128)S(1)}, f32[7,8,128]{2,1,0:T(8,128)S(1)}, u32[]{:S(2)}, u32[]{:S(2)}) collective-permute-start(f32[7,8,128]{2,1,0:T(8,128)S(1)} %get-tuple-element.70), channel_id=1, source_target_pairs={{0,192},{64,0},{128,64},{192,128},{1,193},{65,1},{129,65},{193,129... | collective-permute-start | bytes 86024 | tf_op jit(solution)/shard_map/ppermute | solution.py:462
  81.5 4.0 %collective-permute-start.14 = (f32[8,128]{1,0:T(8,128)S(1)}, f32[8,128]{1,0:T(8,128)S(1)}, u32[]{:S(2)}, u32[]{:S(2)}) collective-permute-start(f32[8,128]{1,0:T(8,128)S(1)} %get-tuple-element.72.refs_12_), channel_id=1, source_target_pairs={{0,128},{64,192},{128,0},{192,64},{1,129},{65,193},{129,1},{193,65... | collective-permute-start | bytes 12296 | tf_op jit(solution)/shard_map/ppermute | solution.py:462

commit v2 on v1

--- a/solution.py
+++ b/solution.py
@@ -69,10 +69,11 @@
 
 
 def pack_kernel(*refs):
-    far, (msg, later, firsts, xlo, xhi), near, (turn, sems) = refs[0:7], refs[7:12], refs[12:18], refs[18:20]
+    far, (msg, later, firsts, stay, leave), near, (turn, sems) = refs[0:7], refs[7:12], refs[12:18], refs[18:20]
     copies = [pltpu.make_async_copy(far[n], near[n], sems.at[n]) for n in (5, 4, 3, 0, 1, 2)]
-    copies.append(pltpu.make_async_copy(far[6].at[:, 0:SY, :], xlo, sems.at[6]))
-    copies.append(pltpu.make_async_copy(far[6].at[:, XY - SY : XY, :], xhi, sems.at[7]))
+    for n, face in enumerate((stay, leave)):
+        start = pl.multiple_of((lax.axis_index("fz") ^ (1 - n)) * (XY - SY), SY)
+        copies.append(pltpu.make_async_copy(far[6].at[:, pl.ds(start, SY), :], face, sems.at[6 + n]))
     for copy in copies:
         copy.start()
     disp, rest, comp, weights, anchor, owner = near
@@ -342,7 +343,7 @@
 
 
 def sample_kernel(t, *refs):
-    viscosity, far_l, far_u = refs[0:3]
+    viscosity, moved, other = refs[0:3]
     refs = refs[2:]
     field, beside_z, xl, xu, yl, yu, wxy, wz = refs[1:9]
     fx = lax.axis_index("fx")
@@ -363,8 +364,12 @@
     u = whole(field)
     below = [jnp.where(me > 0, face, 0.0) for face in whole(yl)]
     above = [jnp.where(me < last, face, 0.0) for face in whole(yu)]
-    before = [jnp.where(fx > 0, far_l[c], 0.0) + part for c, part in enumerate(whole(xl))]
-    after = [jnp.where(fx < lax.axis_size("fx") - 1, far_u[c], 0.0) + part for c, part in enumerate(whole(xu))]
+    first = lax.axis_index("fz") == 0
+    before, after = whole(xl), whole(xu)
+    for c in range(3):
+        far_l, far_u = jnp.where(first, moved[c], other[c]), jnp.where(first, other[c], moved[c])
+        before[c] = before[c] + jnp.where(fx > 0, far_l, 0.0)
+        after[c] = after[c] + jnp.where(fx < lax.axis_size("fx") - 1, far_u, 0.0)
     faces = [before, after, below, above]
     new = wake(u, whole(beside_z), *faces, viscosity[...])
     sampled = sample(new, wxy[...], wz[0])
@@ -470,7 +475,7 @@
     flow = velocity.reshape(3, XY, SZ)
     thick = viscosity.reshape(XY, SZ)
     ins = (disp_init, rest_shape, compliance.reshape(1, SEG_DEV), stencil_weights, anchor, owners)
-    msg, later, _, xlo, xhi = call(
+    msg, later, _, stay, leave = call(
         pack_kernel,
         tuple(pltpu.with_memory_space_constraint(a, pltpu.HBM) for a in (*ins, flow)),
         [shape(GROUP, EARLY), shape(56, SEG_DEV), shape(24, SEG_DEV), shape(3, SY, SZ), shape(3, SY, SZ)],
@@ -479,8 +484,11 @@
         pltpu.HBM,
     )
     static = exchange(msg, ("fx", "fz"))
-    far_l = shifted(xhi, "fx", 1)
-    far_u = shifted(xlo, "fx", -1)
+    both = jnp.concatenate([stay, shifted(leave, "fz", 1)], axis=0)
+    fx_n = lax.axis_size("fx")
+    moves = [(2 * i + f, 2 * ((i + 1 - 2 * f) % fx_n) + f) for i in range(fx_n) for f in range(2)]
+    moved = lax.ppermute(both, ("fx", "fz"), moves)
+    other = shifted(moved[3:6], "fz", 1)
     keep, give, place = call(
         pack_later_kernel,
         (later,),
@@ -521,7 +529,7 @@
         beside_z = shifted(field, "fz", 1)
         if t == 2:
             across = shifted(extra[1], "cable", 2)
-        ins = [thick, far_l, far_u, field, beside_z, xl, xu, yl, yu, *tabled[0:2], *extra]
+        ins = [thick, moved, other, field, beside_z, xl, xu, yl, yu, *tabled[0:2], *extra]
         kernel = functools.partial(sample_kernel, t)
         if t < 2:
             if t == 0:

time: 107 us -> 110 us (1.028)
  blocking collectives: 68.2 us -> 45.8 us
  waiting for transfers between devices: 3.44 us -> 16.2 us
  starting transfers between devices: 24.5 us -> 36.2 us
    all_to_all x4 -> x3, blocking collectives: 68.2 us -> 45.8 us  [exchange(): return lax.all_to_all(array, axes, 0, 0, tiled=True)]
    all_to_all x0 -> x1, starting transfers between devices: none -> 13 us  [exchange(): return lax.all_to_all(array, axes, 0, 0, tiled=True)]
    all_to_all x0 -> x1, waiting for transfers between devices: none -> 9.55 us  [exchange(): return lax.all_to_all(array, axes, 0, 0, tiled=True)]
    ppermute x15, starting transfers between devices: 24.5 us -> 22.3 us  [shifted(): lax.ppermute(array, axis, [(i, (i + by) % count) for i in range(count)])]
    ppermute x0 -> x1, waiting for transfers between devices: none -> 2.11 us  [body(): moved = lax.ppermute(both, ('fx', 'fz'), moves)]
  transfers between devices with their start and end apart: 15 -> 17, of which waited for: 5 -> 8; matrix products, arithmetic and copies ran while one was open for 0% -> 0% of each run, Pallas kernels for 3% -> 4%
where the time goes in v2:
time: 110 us; the launch traced here: 109 us
  blocking collectives  45.8 us (42%)
  starting transfers between devices  36.2 us (33%)
  waiting for transfers between devices  16.2 us (15%)
  Pallas kernels  9.32 us (8%)
  local copies, waits for them, and re-layouts  1.21 us (1%)
    all_to_all x3, blocking collectives, exchange(): return lax.all_to_all(array, axes, 0, 0, tiled=True)  45.8 us
    ppermute x15, starting transfers between devices, shifted(): lax.ppermute(array, axis, [(i, (i + by) % count) for i in range(count)])  22.3 us
    all_to_all x1, starting transfers between devices, exchange(): return lax.all_to_all(array, axes, 0, 0, tiled=True)  13 us
    all_to_all x1, waiting for transfers between devices, exchange(): return lax.all_to_all(array, axes, 0, 0, tiled=True)  9.55 us
    pallas_call x14, Pallas kernels, call(): pl.pallas_call(kernel, out_shape=outs, in_specs=[pl.BlockSpec(memory_spac...  9.32 us
    ppermute x15, waiting for transfers between devices, shifted(): lax.ppermute(array, axis, [(i, (i + by) % count) for i in range(count)])  4.51 us
  transfers between devices with their start and end apart: 17, of which 8 were waited for; matrix products, arithmetic and copies ran while one was open for 0% of the time, Pallas kernels for 4%

profile of v2, /device:TPU:1, one launch (start us, length us, event | category | flops | bytes accessed | tf_op | source)
XLA Modules:
  0.0 109.5 jit_solution(15192174804901389951)
XLA Ops:
  0.6 1.5 %shard_map.95 = (f32[64,256]{1,0:T(8,128)S(1)}, f32[56,64]{1,0:T(8,128)S(1)}, f32[24,64]{1,0:T(8,128)}, f32[3,16,128]{2,1,0:T(8,128)S(1)}, f32[3,16,128]{2,1,0:T(8,128)S(1)}) custom-call(f32[3,64]{1,0:T(4,128)} %refs_0_.1, f32[3,64]{1,0:T(4,128)} %refs_1_.1, f32[1,64]{1,0:T(1,128)} %bitcast.43, f32[3,12,64]{2,1,0:T(8,128)} %refs_3_.1, s32[3,64]{1,0:T(4,128)} %refs_4_.1, ...), custom_call_target="tpu_custom_call" | custom-call | bytes 344320 | tf_op jit(solution)/shard_map/pallas_call | solution.py:454
  2.2 0.0 copy-start
  2.2 0.7 copy.10
  2.9 13.0 %all-to-all-start = ((f32[64,1,256]{2,1,0:T(1,128)}), f32[64,1,256]{2,1,0:T(1,128)S(1)}, u32[]{:S(2)}, u32[]{:S(2)}) async-start(f32[64,1,256]{2,1,0:T(1,128)} %copy.10), calls=%async_computation | async-start | bytes 131072 | tf_op jit(solution)/shard_map/all_to_all | solution.py:471
  15.9 0.5 collective-permute-start
  16.4 9.5 %all-to-all-done = f32[64,1,256]{2,1,0:T(1,128)S(1)} async-done(((f32[64,1,256]{2,1,0:T(1,128)}), f32[64,1,256]{2,1,0:T(1,128)S(1)}, u32[]{:S(2)}, u32[]{:S(2)}) %all-to-all-start) | async-done | bytes 65568 | tf_op jit(solution)/shard_map/all_to_all | solution.py:471
  26.0 0.8 shard_map.96
  26.8 0.4 collective-permute-start.3
  27.2 0.6 shard_map.98
  27.8 0.2 collective-permute-start.6
  28.0 0.9 collective-permute-start.1
  28.9 2.1 %collective-permute-done.1.refs_1_ = f32[6,16,128]{2,1,0:T(8,128)S(1)} collective-permute-done((f32[6,16,128]{2,1,0:T(8,128)S(1)}, f32[6,16,128]{2,1,0:T(8,128)S(1)}, u32[]{:S(2)}, u32[]{:S(2)}) %collective-permute-start.1) | collective-permute-done | bytes 49184 | tf_op jit(solution)/shard_map/ppermute | solution.py:490
  31.0 4.9 %collective-permute-start.2 = (f32[3,16,128]{2,1,0:T(8,128)S(1)}, f32[3,16,128]{2,1,0:T(8,128)S(1)}, u32[]{:S(2)}, u32[]{:S(2)}) collective-permute-start(f32[3,16,128]{2,1,0:T(8,128)S(1)} %slice.8), channel_id=1, source_target_pairs={{0,1},{1,0},{2,3},{3,2},{4,5},{5,4},{6,7},{7,6},{8,9},{9,8},{10,11... | collective-permute-start | bytes 73736 | tf_op jit(solution)/shard_map/ppermute | solution.py:467
  35.9 1.3 %collective-permute-start.4 = (f32[3,8,128]{2,1,0:T(8,128)S(1)}, f32[3,8,128]{2,1,0:T(8,128)S(1)}, u32[]{:S(2)}, u32[]{:S(2)}) collective-permute-start(f32[3,8,128]{2,1,0:T(8,128)S(1)} %get-tuple-element.45), channel_id=1, source_target_pairs={{0,64},{64,128},{128,192},{192,0},{1,65},{65,129},{129,193},{193,1... | collective-permute-start | bytes 36872 | tf_op jit(solution)/shard_map/ppermute | solution.py:467
  37.2 1.4 %collective-permute-start.5 = (f32[3,8,128]{2,1,0:T(8,128)S(1)}, f32[3,8,128]{2,1,0:T(8,128)S(1)}, u32[]{:S(2)}, u32[]{:S(2)}) collective-permute-start(f32[3,8,128]{2,1,0:T(8,128)S(1)} %get-tuple-element.46), channel_id=1, source_target_pairs={{0,192},{64,0},{128,64},{192,128},{1,193},{65,1},{129,65},{193,129... | collective-permute-start | bytes 36872 | tf_op jit(solution)/shard_map/ppermute | solution.py:467
  38.6 0.5 shard_map.97
  39.1 0.0 collective-permute-done.6.refs_12_
  39.2 0.6 collective-permute-done.4.refs_7_
  39.7 0.3 collective-permute-done.5.refs_8_
  40.0 0.4 shard_map.99
  40.4 0.3 copy.11
  40.7 14.1 %all_to_all.44 = f32[32,1,2048]{2,1,0:T(1,128)S(1)} all-to-all(f32[32,1,2048]{2,1,0:T(1,128)S(1)} %copy.11), channel_id=1, replica_groups=mesh['cable'=4,'fx'=32,'fz'=2] {'fx'}, dimensions={0} | all-to-all | bytes 524288 | tf_op jit(solution)/shard_map/all_to_all | solution.py:471
  54.8 0.1 copy.20
  54.9 3.0 %collective-permute-start.7 = (f32[32,768]{1,0:T(8,128)S(1)}, f32[32,768]{1,0:T(8,128)S(1)}, u32[]{:S(2)}, u32[]{:S(2)}) collective-permute-start(f32[32,768]{1,0:T(8,128)S(1)} %slice.9), channel_id=1, source_target_pairs={{0,1},{1,0},{2,3},{3,2},{4,5},{5,4},{6,7},{7,6},{8,9},{9,8},{10,11... | collective-permute-start | bytes 294920 | tf_op jit(solution)/shard_map/ppermute | solution.py:467
  57.9 0.4 shard_map.100
  58.3 0.6 collective-permute-done.7.refs_2_.refs_1_
  58.9 0.5 shard_map.101
  59.3 0.4 collective-permute-start.8
  59.8 1.0 collective-permute-start.9
  60.8 1.7 %collective-permute-start.10 = (f32[3,8,128]{2,1,0:T(8,128)S(1)}, f32[3,8,128]{2,1,0:T(8,128)S(1)}, u32[]{:S(2)}, u32[]{:S(2)}) collective-permute-start(f32[3,8,128]{2,1,0:T(8,128)S(1)} %get-tuple-element.60), channel_id=1, source_target_pairs={{0,192},{64,0},{128,64},{192,128},{1,193},{65,1},{129,65},{193,129... | collective-permute-start | bytes 36872 | tf_op jit(solution)/shard_map/ppermute | solution.py:467
  62.5 0.5 shard_map.102
  63.0 0.6 collective-permute-done.9.refs_7_
  63.6 0.5 shard_map.103
  64.0 0.1 copy.12
  64.2 12.4 %all_to_all.45 = f32[32,1,896]{2,1,0:T(1,128)S(1)} all-to-all(f32[32,1,896]{2,1,0:T(1,128)S(1)} %copy.12), channel_id=1, replica_groups=mesh['cable'=4,'fx'=32,'fz'=2] {'fx'}, dimensions={0} | all-to-all | bytes 229376 | tf_op jit(solution)/shard_map/all_to_all | solution.py:471
  76.5 2.9 %collective-permute-start.11 = (f32[32,896]{1,0:T(8,128)S(1)}, f32[32,896]{1,0:T(8,128)S(1)}, u32[]{:S(2)}, u32[]{:S(2)}) collective-permute-start(f32[32,896]{1,0:T(8,128)S(1)} %bitcast.31), channel_id=1, source_target_pairs={{0,1},{1,0},{2,3},{3,2},{4,5},{5,4},{6,7},{7,6},{8,9},{9,8},{10,11... | collective-permute-start | bytes 344072 | tf_op jit(solution)/shard_map/ppermute | solution.py:467
  79.5 0.8 shard_map.104
  80.2 0.2 collective-permute-done.11.refs_2_.refs_1_
  80.4 0.6 shard_map.105
  81.0 0.4 collective-permute-start.12
  81.5 1.0 collective-permute-start.13
  82.5 1.9 %collective-permute-start.14 = (f32[7,8,128]{2,1,0:T(8,128)S(1)}, f32[7,8,128]{2,1,0:T(8,128)S(1)}, u32[]{:S(2)}, u32[]{:S(2)}) collective-permute-start(f32[7,8,128]{2,1,0:T(8,128)S(1)} %get-tuple-element.70), channel_id=1, source_target_pairs={{0,192},{64,0},{128,64},{192,128},{1,193},{65,1},{129,65},{193,129... | collective-permute-start | bytes 86024 | tf_op jit(solution)/shard_map/ppermute | solution.py:467
  84.3 1.2 %collective-permute-start.15 = (f32[8,128]{1,0:T(8,128)S(1)}, f32[8,128]{1,0:T(8,128)S(1)}, u32[]{:S(2)}, u32[]{:S(2)}) collective-permute-start(f32[8,128]{1,0:T(8,128)S(1)} %get-tuple-element.72.refs_12_), channel_id=1, source_target_pairs={{0,128},{64,192},{128,0},{192,64},{1,129},{65,193},{129,1},{193,65... | collective-permute-start | bytes 12296 | tf_op jit(solution)/shard_map/ppermute | solution.py:467
  85.5 0.5 shard_map.106
  86.1 2.3 %collective-permute-done.15.refs_13_ = f32[8,128]{1,0:T(8,128)S(1)} collective-permute-done((f32[8,128]{1,0:T(8,128)S(1)}, f32[8,128]{1,0:T(8,128)S(1)}, u32[]{:S(2)}, u32[]{:S(2)}) %collective-permute-start.15) | collective-permute-done | bytes 4128 | tf_op jit(solution)/shard_map/ppermute | solution.py:467
  88.3 1.0 shard_map.107
  89.4 19.3 %all_to_all.46 = f32[256,1,128]{2,1,0:T(1,128)S(1)} all-to-all(f32[256,1,128]{2,1,0:T(1,128)S(1)} %bitcast.41), channel_id=1, replica_groups=mesh['cable'=4,'fx'=32,'fz'=2] {'cable','fx','fz'}, dimensions={0} | all-to-all | bytes 262144 | tf_op jit(solution)/shard_map/all_to_all | solution.py:471
  108.6 0.8 shard_map.108
  (16 shorter events, 0.1 us)
Async XLA Ops:
  2.2 23.8 %copy-start = (f32[3,8,16,128]{3,2,1,0:T(8,128)S(1)}, f32[3,8,16,128]{3,2,1,0:T(8,128)}, u32[]{:S(2)}) copy-start(f32[3,8,16,128]{3,2,1,0:T(8,128)} %param.8) | copy-start | bytes 589828
  2.9 23.1 %all-to-all-start = ((f32[64,1,256]{2,1,0:T(1,128)}), f32[64,1,256]{2,1,0:T(1,128)S(1)}, u32[]{:S(2)}, u32[]{:S(2)}) async-start(f32[64,1,256]{2,1,0:T(1,128)} %copy.10), calls=%async_computation | async-start | bytes 131072 | tf_op jit(solution)/shard_map/all_to_all | solution.py:471
  15.9 12.1 %collective-permute-start = (f32[3,16,128]{2,1,0:T(8,128)S(1)}, f32[3,16,128]{2,1,0:T(8,128)S(1)}, u32[]{:S(2)}, u32[]{:S(2)}) collective-permute-start(f32[3,16,128]{2,1,0:T(8,128)S(1)} %get-tuple-element.40), channel_id=1, source_target_pairs={{0,1},{1,0},{2,3},{3,2},{4,5},{5,4},{6,7},{7,6},{8,9},{9,8},{10,11... | collective-permute-start | bytes 73736 | tf_op jit(solution)/shard_map/ppermute | solution.py:467
  26.8 13.3 %collective-permute-start.3 = (f32[3,128,128]{2,1,0:T(8,128)S(1)}, f32[3,128,128]{2,1,0:T(8,128)S(1)}, u32[]{:S(2)}, u32[]{:S(2)}) collective-permute-start(f32[3,128,128]{2,1,0:T(8,128)S(1)} %get-tuple-element.42.refs_3_), channel_id=1, source_target_pairs={{0,1},{1,0},{2,3},{3,2},{4,5},{5,4},{6,7},{7,6},{8,9},{9,8},{10,11... | collective-permute-start | bytes 589832 | tf_op jit(solution)/shard_map/ppermute | solution.py:467
  27.8 11.4 %collective-permute-start.6 = (f32[32,640]{1,0:T(8,128)S(1)}, f32[32,640]{1,0:T(8,128)S(1)}, u32[]{:S(2)}, u32[]{:S(2)}) collective-permute-start(f32[32,640]{1,0:T(8,128)S(1)} %get-tuple-element.51), channel_id=1, source_target_pairs={{0,1},{1,0},{2,3},{3,2},{4,5},{5,4},{6,7},{7,6},{8,9},{9,8},{10,11... | collective-permute-start | bytes 245768 | tf_op jit(solution)/shard_map/ppermute | solution.py:467
  28.0 12.0 %copy-start.1 = (f32[8,16,128]{2,1,0:T(8,128)S(1)}, f32[8,16,128]{2,1,0:T(8,128)}, u32[]{:S(2)}) copy-start(f32[8,16,128]{2,1,0:T(8,128)} %param.9) | copy-start | bytes 196612
  28.0 3.0 %collective-permute-start.1 = (f32[6,16,128]{2,1,0:T(8,128)S(1)}, f32[6,16,128]{2,1,0:T(8,128)S(1)}, u32[]{:S(2)}, u32[]{:S(2)}) collective-permute-start(f32[6,16,128]{2,1,0:T(8,128)S(1)} %pad_maximum_fusion), channel_id=1, source_target_pairs={{0,2},{1,63},{2,4},{3,1},{4,6},{5,3},{6,8},{7,5},{8,10},{9,7},{10,... | collective-permute-start | bytes 147464 | tf_op jit(solution)/shard_map/ppermute | solution.py:490
  31.0 8.1 %collective-permute-start.2 = (f32[3,16,128]{2,1,0:T(8,128)S(1)}, f32[3,16,128]{2,1,0:T(8,128)S(1)}, u32[]{:S(2)}, u32[]{:S(2)}) collective-permute-start(f32[3,16,128]{2,1,0:T(8,128)S(1)} %slice.8), channel_id=1, source_target_pairs={{0,1},{1,0},{2,3},{3,2},{4,5},{5,4},{6,7},{7,6},{8,9},{9,8},{10,11... | collective-permute-start | bytes 73736 | tf_op jit(solution)/shard_map/ppermute | solution.py:467
  35.9 3.8 %collective-permute-start.4 = (f32[3,8,128]{2,1,0:T(8,128)S(1)}, f32[3,8,128]{2,1,0:T(8,128)S(1)}, u32[]{:S(2)}, u32[]{:S(2)}) collective-permute-start(f32[3,8,128]{2,1,0:T(8,128)S(1)} %get-tuple-element.45), channel_id=1, source_target_pairs={{0,64},{64,128},{128,192},{192,0},{1,65},{65,129},{129,193},{193,1... | collective-permute-start | bytes 36872 | tf_op jit(solution)/shard_map/ppermute | solution.py:467
  37.2 2.8 %collective-permute-start.5 = (f32[3,8,128]{2,1,0:T(8,128)S(1)}, f32[3,8,128]{2,1,0:T(8,128)S(1)}, u32[]{:S(2)}, u32[]{:S(2)}) collective-permute-start(f32[3,8,128]{2,1,0:T(8,128)S(1)} %get-tuple-element.46), channel_id=1, source_target_pairs={{0,192},{64,0},{128,64},{192,128},{1,193},{65,1},{129,65},{193,129... | collective-permute-start | bytes 36872 | tf_op jit(solution)/shard_map/ppermute | solution.py:467
  54.9 4.0 %collective-permute-start.7 = (f32[32,768]{1,0:T(8,128)S(1)}, f32[32,768]{1,0:T(8,128)S(1)}, u32[]{:S(2)}, u32[]{:S(2)}) collective-permute-start(f32[32,768]{1,0:T(8,128)S(1)} %slice.9), channel_id=1, source_target_pairs={{0,1},{1,0},{2,3},{3,2},{4,5},{5,4},{6,7},{7,6},{8,9},{9,8},{10,11... | collective-permute-start | bytes 294920 | tf_op jit(solution)/shard_map/ppermute | solution.py:467
  59.3 4.2 %collective-permute-start.8 = (f32[3,128,128]{2,1,0:T(8,128)S(1)}, f32[3,128,128]{2,1,0:T(8,128)S(1)}, u32[]{:S(2)}, u32[]{:S(2)}) collective-permute-start(f32[3,128,128]{2,1,0:T(8,128)S(1)} %get-tuple-element.56.refs_3_), channel_id=1, source_target_pairs={{0,1},{1,0},{2,3},{3,2},{4,5},{5,4},{6,7},{7,6},{8,9},{9,8},{10,11... | collective-permute-start | bytes 589832 | tf_op jit(solution)/shard_map/ppermute | solution.py:467
  59.8 3.8 %collective-permute-start.9 = (f32[3,8,128]{2,1,0:T(8,128)S(1)}, f32[3,8,128]{2,1,0:T(8,128)S(1)}, u32[]{:S(2)}, u32[]{:S(2)}) collective-permute-start(f32[3,8,128]{2,1,0:T(8,128)S(1)} %get-tuple-element.59), channel_id=1, source_target_pairs={{0,64},{64,128},{128,192},{192,0},{1,65},{65,129},{129,193},{193,1... | collective-permute-start | bytes 36872 | tf_op jit(solution)/shard_map/ppermute | solution.py:467
  60.8 2.8 %collective-permute-start.10 = (f32[3,8,128]{2,1,0:T(8,128)S(1)}, f32[3,8,128]{2,1,0:T(8,128)S(1)}, u32[]{:S(2)}, u32[]{:S(2)}) collective-permute-start(f32[3,8,128]{2,1,0:T(8,128)S(1)} %get-tuple-element.60), channel_id=1, source_target_pairs={{0,192},{64,0},{128,64},{192,128},{1,193},{65,1},{129,65},{193,129... | collective-permute-start | bytes 36872 | tf_op jit(solution)/shard_map/ppermute | solution.py:467
  76.5 3.9 %collective-permute-start.11 = (f32[32,896]{1,0:T(8,128)S(1)}, f32[32,896]{1,0:T(8,128)S(1)}, u32[]{:S(2)}, u32[]{:S(2)}) collective-permute-start(f32[32,896]{1,0:T(8,128)S(1)} %bitcast.31), channel_id=1, source_target_pairs={{0,1},{1,0},{2,3},{3,2},{4,5},{5,4},{6,7},{7,6},{8,9},{9,8},{10,11... | collective-permute-start | bytes 344072 | tf_op jit(solution)/shard_map/ppermute | solution.py:467
  81.0 7.3 %collective-permute-start.12 = (f32[6,128,128]{2,1,0:T(8,128)S(1)}, f32[6,128,128]{2,1,0:T(8,128)S(1)}, u32[]{:S(2)}, u32[]{:S(2)}) collective-permute-start(f32[6,128,128]{2,1,0:T(8,128)S(1)} %get-tuple-element.66.refs_3_), channel_id=1, source_target_pairs={{0,1},{1,0},{2,3},{3,2},{4,5},{5,4},{6,7},{7,6},{8,9},{9,8},{10,11... | collective-permute-start | bytes 1179656 | tf_op jit(solution)/shard_map/ppermute | solution.py:467
  81.5 6.9 %collective-permute-start.13 = (f32[7,8,128]{2,1,0:T(8,128)S(1)}, f32[7,8,128]{2,1,0:T(8,128)S(1)}, u32[]{:S(2)}, u32[]{:S(2)}) collective-permute-start(f32[7,8,128]{2,1,0:T(8,128)S(1)} %get-tuple-element.69), channel_id=1, source_target_pairs={{0,64},{64,128},{128,192},{192,0},{1,65},{65,129},{129,193},{193,1... | collective-permute-start | bytes 86024 | tf_op jit(solution)/shard_map/ppermute | solution.py:467
  82.5 5.8 %collective-permute-start.14 = (f32[7,8,128]{2,1,0:T(8,128)S(1)}, f32[7,8,128]{2,1,0:T(8,128)S(1)}, u32[]{:S(2)}, u32[]{:S(2)}) collective-permute-start(f32[7,8,128]{2,1,0:T(8,128)S(1)} %get-tuple-element.70), channel_id=1, source_target_pairs={{0,192},{64,0},{128,64},{192,128},{1,193},{65,1},{129,65},{193,129... | collective-permute-start | bytes 86024 | tf_op jit(solution)/shard_map/ppermute | solution.py:467
  84.3 4.0 %collective-permute-start.15 = (f32[8,128]{1,0:T(8,128)S(1)}, f32[8,128]{1,0:T(8,128)S(1)}, u32[]{:S(2)}, u32[]{:S(2)}) collective-permute-start(f32[8,128]{1,0:T(8,128)S(1)} %get-tuple-element.72.refs_12_), channel_id=1, source_target_pairs={{0,128},{64,192},{128,0},{192,64},{1,129},{65,193},{129,1},{193,65... | collective-permute-start | bytes 12296 | tf_op jit(solution)/shard_map/ppermute | solution.py:467
